TPU v7x, 128 devices: a whole 4x4x4 slice. The times are simulated.
128 devices in a mesh: gz: 128 (over x, y, z, core).
Axes of the slice: x: 4, y: 4, z: 4, core: 2. Of those that a mesh axis runs over, the one named last changes fastest.
Arguments:
- moments: float32 [10, 1024, 128, 128], P(None, 'gz')
- shapes: float32 [1024, 3, 289], P('gz'), may hold values from -0.6 to 0.6
- anchors: int32 [1024, 3], P('gz'), may hold values from 0 to 1023, as said below
- synthesis: float32 [512, 289], replicated, may hold values from -6 to 6
- spreading: float32 [512, 2048], replicated, may hold values from 0 to 0.001953125
Outputs:
- moments_out: float32 [10, 1024, 128, 128], P(None, 'gz')
- shapes_out: float32 [1024, 3, 289], P('gz')
Inputs may be any that keep to these rules, and one draw needn't show every extreme that they name: `anchors`: membrane m is owned by device m // 8; the slab of its box's first plane (anchor_z // 8) is its owner's, the one before or the one after, cyclically over 1024 planes. Rows and columns lie below 128.
All inputs are finite; a program needn't handle non-finite values.
Results may differ from a plain program's by a relative error of at most 0.00017.
Values sent between devices are 32-bit elements; how exact they have to be, the bound alone decides.
No kernel may reach another device: no remote copies, remote signals or barrier semaphores. Data moves between devices by JAX's collectives and lax.ppermute only.
A program may use at most 256 MiB of HBM per device.

v0:
```python
import functools

import jax
import jax.numpy as jnp
from jax import lax
from jax.experimental import pallas as pl
from jax.experimental.pallas import tpu as pltpu
from jax.sharding import PartitionSpec as P

LMAX = 16
BZ = 8
BXY = 16
STEPS = 3
STIFF_SCALE = 0.002
MOBILITY = 0.5

PLANES = 8
SIDE = 128
OWNED = 8
COEFS = 289
LANES = 384
CELLS = 2048
POINTS = 512
GROUP = OWNED * 3
BLOCKS = 5
ROWS = GROUP * BLOCKS
ANCHOR_LANE = 300
FIELDS = 10
PADDED = 144
PITCH = 145
DEPTH = PLANES + 2 * BZ
BOXED = ROWS + 1
CHUNK = 16
JK = ((0, 0), (1, 0), (2, 0), (0, 1), (1, 1), (0, 2))

ANY = pl.BlockSpec(memory_space=pl.ANY)
VMEM = pl.BlockSpec(memory_space=pltpu.VMEM)
SMEM = pl.BlockSpec(memory_space=pltpu.SMEM)
F32 = jnp.float32
BF16 = jnp.bfloat16


def shifted(block, distance):
    devices = lax.axis_size("gz")
    return lax.ppermute(block, "gz", [((i - distance) % devices, i) for i in range(devices)])


def split(value):
    high = value.astype(BF16)
    return high, (value - high.astype(F32)).astype(BF16)


def place(group):
    return group // 5, (group % 5) * GROUP


def chunk_row(n):
    return (n % 2 * 8 + n // 2) * BOXED


def couple_kernel(synthesis_ref, spreading_ref, high_ref, low_ref):
    s_high, s_low = split(synthesis_ref[...])
    w_high, w_low = split(spreading_ref[...])
    dot = functools.partial(
        lax.dot_general, dimension_numbers=(((0,), (0,)), ((), ())), preferred_element_type=F32
    )
    total = dot(s_high, w_high) + (dot(s_high, w_low) + dot(s_low, w_high))
    high, low = split(total)
    high_ref[...] = high
    low_ref[...] = low


def couple(synthesis, spreading):
    width = 512
    shape = jax.ShapeDtypeStruct((LANES, CELLS), BF16)
    return pl.pallas_call(
        couple_kernel,
        out_shape=(shape, shape),
        grid=(CELLS // width,),
        in_specs=[
            pl.BlockSpec((POINTS, LANES), lambda i: (0, 0)),
            pl.BlockSpec((POINTS, width), lambda i: (0, i)),
        ],
        out_specs=[pl.BlockSpec((LANES, width), lambda i: (0, i))] * 2,
        cost_estimate=pl.CostEstimate(
            flops=6 * LANES * POINTS * CELLS, bytes_accessed=8 * 2**20, transcendentals=0
        ),
        name="couple",
    )(synthesis, spreading)


def pack_kernel(first_ref, last_ref, small_ref, up_ref, down_ref):
    for out_ref, plane_ref in ((up_ref, last_ref), (down_ref, first_ref)):
        out_ref[0:FIELDS] = plane_ref[:, 0]
        for part in range(3):
            block, row = place(part)
            out_ref[FIELDS + block, row : row + GROUP] = small_ref[:, part * 128 : part * 128 + 128]


def pack(moments, small):
    shape = jax.ShapeDtypeStruct((FIELDS + 1, SIDE, SIDE), F32)
    whole = pl.BlockSpec((FIELDS + 1, SIDE, SIDE), lambda i: (0, 0, 0))
    return pl.pallas_call(
        pack_kernel,
        out_shape=(shape, shape),
        grid=(1,),
        in_specs=[
            pl.BlockSpec((FIELDS, 1, SIDE, SIDE), lambda i: (0, 0, 0, 0)),
            pl.BlockSpec((FIELDS, 1, SIDE, SIDE), lambda i: (0, PLANES - 1, 0, 0)),
            pl.BlockSpec((GROUP, LANES), lambda i: (0, 0)),
        ],
        out_specs=[whole, whole],
        name="pack",
    )(moments, moments, small)


def spread_x(zero, one, two):
    plus = zero if two is None else zero + two
    minus = plus
    if one is not None:
        plus, minus = plus + one, plus - one
    plus = pltpu.roll(plus, 1, 1)
    minus = pltpu.roll(minus, SIDE - 1, 1)
    both = plus + minus
    return (4.0 * zero + both, plus - minus, both)


def collide_rows(m, force):
    unit = 1.0 / 216.0
    rho = m[0]
    u = [m[1 + a] + 0.5 * force[a] for a in range(3)]
    t = [0.625 * u[a] + 0.375 * force[a] for a in range(3)]
    v = [(9.0 * unit) * u[a] for a in range(3)]
    line = [(3.0 * unit) * (m[1 + a] + force[a]) for a in range(3)]
    shared = (0.375 * unit) * rho
    square = [shared - (1.125 * unit) * m[4 + a] + v[a] * t[a] for a in range(3)]
    cross = [
        v[a] * t[b] + v[b] * t[a] - (2.25 * unit) * m[7 + n]
        for n, (a, b) in enumerate(((0, 1), (0, 2), (1, 2)))
    ]
    cell = unit * rho - (1.0 / 3.0) * (square[0] + square[1] + square[2])
    return cell, line, square, cross


def step_kernel(first, last, *refs):
    refs = list(refs)
    slots_ref = refs.pop(0)
    high_ref, low_ref, moments_hbm, up_hbm, down_hbm = refs[:5]
    del refs[:5]
    if first:
        own_ref, below_ref, above_ref = refs[:3]
        del refs[:3]
    else:
        state_ref, sum_ref = refs[:2]
        del refs[:2]
    out_hbm, newsum_ref = refs[:2]
    del refs[:2]
    if not last:
        newstate_ref, sendup_hbm, senddown_hbm = refs[:3]
        del refs[:3]
    (
        old, new, velocity, force, boxes, sampled, tail_up, tail_down,
        shifts, stills, ring, middle, state,
        in_sem, halo_sem, out_sem, send_sem,
    ) = refs

    up_blocks = up_hbm.shape[0] - FIELDS
    down_blocks = down_hbm.shape[0] - FIELDS
    fetch_tails = [
        pltpu.make_async_copy(up_hbm.at[pl.ds(FIELDS, up_blocks)], tail_up.at[pl.ds(0, up_blocks)], halo_sem.at[0]),
        pltpu.make_async_copy(down_hbm.at[pl.ds(FIELDS, down_blocks)], tail_down.at[pl.ds(0, down_blocks)], halo_sem.at[1]),
    ]
    fetch_planes = [pltpu.make_async_copy(up_hbm.at[pl.ds(0, FIELDS)], old.at[:, 0], in_sem.at[0])]
    for z in range(PLANES):
        fetch_planes.append(
            pltpu.make_async_copy(moments_hbm.at[:, z], old.at[:, z + 1], in_sem.at[z + 1])
        )
    fetch_planes.append(
        pltpu.make_async_copy(down_hbm.at[pl.ds(0, FIELDS)], old.at[:, PLANES + 1], in_sem.at[PLANES + 1])
    )
    for copy in fetch_tails:
        copy.start()
    for copy in fetch_planes:
        copy.start()

    for c in range(3):
        start = (c * DEPTH + BZ - 1) * PITCH
        force[start : start + (PLANES + 2) * PITCH] = jnp.zeros(((PLANES + 2) * PITCH, SIDE), F32)
    sampled[...] = jnp.zeros_like(sampled)
    for copy in fetch_tails:
        copy.wait()

    for part in range(3):
        lanes = slice(part * 128, part * 128 + 128)

        def tail(ref, owner):
            block, row = place(owner * 3 + part)
            return ref[block, row : row + GROUP]

        for owner in range(BLOCKS):
            rows = slice(owner * GROUP, owner * GROUP + GROUP)
            if first:
                value = (
                    below_ref[:, lanes] if owner == 0
                    else tail(tail_up, 0) if owner == 1
                    else own_ref[:, lanes] if owner == 2
                    else tail(tail_down, 0) if owner == 3
                    else above_ref[:, lanes]
                )
                if part == 2:
                    lane = lax.broadcasted_iota(jnp.int32, value.shape, 1)
                    value = jnp.where(lane < COEFS - 256, value, 0.0)
            else:
                value = state_ref[rows, lanes]
                if owner < 3:
                    value = value + MOBILITY * tail(tail_up, owner)
                if owner > 0:
                    value = value + MOBILITY * tail(tail_down, owner - 1)
            state[rows, lanes] = value

    number = lax.broadcasted_iota(jnp.int32, (1, LANES), 1)
    degree = jnp.zeros((1, LANES), jnp.int32)
    for step in range(1, LMAX + 1):
        degree = degree + (number >= step * step).astype(jnp.int32)
    stiffness = STIFF_SCALE * (degree * (degree + 1) + 2).astype(F32)
    coef_high, coef_low = split(-stiffness * state[...])
    both = jnp.concatenate([coef_high, coef_low], axis=0)
    for part in range(CELLS // 512):
        lanes = slice(part * 512, part * 512 + 512)
        main = jnp.dot(both, high_ref[:, lanes], preferred_element_type=F32)
        rest = jnp.dot(coef_high, low_ref[:, lanes], preferred_element_type=F32)
        whole = main[:ROWS] + (main[ROWS:] + rest)
        for chunk in range(4):
            start = chunk_row(part * 4 + chunk)
            boxes[start : start + ROWS] = whole[:, chunk * 128 : chunk * 128 + 128]

    def box_parts(slot):
        above = slots_ref[slot * 3]
        row = slots_ref[slot * 3 + 1]
        column = slots_ref[slot * 3 + 2]
        lane = lax.broadcasted_iota(jnp.int32, (BXY, SIDE), 1)
        inside = lax.broadcasted_iota(jnp.int32, (BXY, SIDE), 0)
        hit = (((lane - column) & (SIDE - 1)) == inside).astype(F32).astype(BF16)
        none = jnp.zeros((BXY, SIDE), BF16)
        spots = jnp.concatenate(
            [jnp.concatenate([hit if i == n else none for i in range(8)], axis=1) for n in range(8)],
            axis=0,
        )
        starts = [
            (c * DEPTH + above + BZ) * PITCH + row + half * 8 for c in range(3) for half in range(2)
        ]
        rows = [half * 8 * BOXED + slot * 3 + c for c in range(3) for half in range(2)]
        return above, spots, starts, rows

    def place_box(slot, carry):
        @pl.when(jnp.logical_and(slots_ref[slot * 3] >= -BZ, slots_ref[slot * 3] <= PLANES))
        def _():
            above, spots, starts, rows = box_parts(slot)
            cells = jnp.concatenate([boxes[pl.ds(start, 8, stride=BOXED)] for start in rows], axis=0)
            placed = jnp.dot(
                jnp.concatenate(split(cells), axis=1),
                jnp.concatenate([spots, spots], axis=0),
                preferred_element_type=F32,
            )
            where = [
                (pl.ds(start + i, 8, stride=PITCH), slice(n * 8, n * 8 + 8), slice(i * 128, i * 128 + 128))
                for n, start in enumerate(starts)
                for i in range(8)
            ]
            sums = [force[there] + placed[here, lanes] for there, here, lanes in where]
            for (there, here, lanes), value in zip(where, sums):
                force[there] = value

        return carry

    lax.fori_loop(0, BLOCKS * OWNED, place_box, 0)

    def fold(z, carry):
        for c in range(3):
            start = (c * DEPTH + z + BZ - 1) * PITCH
            first = pl.ds(start, BXY)
            force[first] = force[first] + force[pl.ds(start + SIDE, BXY)]
        return carry

    lax.fori_loop(0, PLANES + 2, fold, 0)

    def stream_plane(z, carry):
        pltpu.make_async_copy(moments_hbm.at[:, 0], old.at[:, z], in_sem.at[z]).wait()

        def collide_chunk(step, carry):
            y = pl.multiple_of(step * CHUNK, CHUNK)
            rows = pl.ds(y, CHUNK)
            m = [old[f, z, rows] for f in range(FIELDS)]
            cell, line, square, cross = collide_rows(
                m, [force[pl.ds((c * DEPTH + z + BZ - 1) * PITCH + y, CHUNK)] for c in range(3)]
            )
            even = [
                spread_x(cell, line[2], square[2]),
                spread_x(line[1], cross[2], None),
                spread_x(square[1], None, None),
            ]
            twice = spread_x(square[0], None, None)
            odd = [spread_x(line[0], cross[1], None), spread_x(cross[0], None, None)]
            moved = pl.ds(y + 8, CHUNK)
            for k in range(3):
                ends = even[0][k] + even[2][k]
                shifts[k, moved] = ends + even[1][k]
                shifts[3 + k, moved] = ends - even[1][k]
                shifts[6 + k, moved] = odd[0][k] + odd[1][k]
                shifts[9 + k, moved] = odd[0][k] - odd[1][k]
                shifts[12 + k, moved] = twice[k]
                stills[k, rows] = 4.0 * even[0][k]
                stills[3 + k, rows] = 4.0 * odd[0][k]
            return carry

        lax.fori_loop(0, SIDE // CHUNK, collide_chunk, 0)
        for field in range(15):
            shifts[field, 7:8] = shifts[field, SIDE + 7 : SIDE + 8]
            shifts[field, SIDE + 8 : SIDE + 9] = shifts[field, 8:9]
        parity = z % 2
        inner = jnp.clip(z - 2, 0, PLANES - 1)

        for step in range(SIDE // CHUNK):
            y = step * CHUNK
            rows = slice(y, y + CHUNK)
            after = slice(y + 7, y + 7 + CHUNK)
            before = slice(y + 9, y + 9 + CHUNK)
            even, odd, twice = {}, {}, {}
            for k in range(3):
                for target, plus, minus, still in (
                    (even, k, 3 + k, lambda k=k: stills[k, rows]),
                    (odd, 6 + k, 9 + k, lambda k=k: stills[3 + k, rows]),
                    (twice, 12 + k, 12 + k, lambda k=k: 4.0 * shifts[12 + k, y + 8 : y + 8 + CHUNK]),
                ):
                    up, down = shifts[plus, after], shifts[minus, before]
                    both = up + down
                    target[0, k] = still() + both
                    if k < 2:
                        target[1, k] = up - down
                    if k < 1:
                        target[2, k] = both
            total, difference, centre = {}, {}, {}
            for n, key in enumerate(JK):
                ends = even[key] + twice[key]
                under = ring[parity, n, rows]
                over = ends - odd[key]
                total[key] = under + over
                difference[key] = under - over
                centre[key] = middle[n, rows] + total[key]
                ring[parity, n, rows] = ends + odd[key]
                middle[n, rows] = 4.0 * even[key]
            flow = (difference[0, 0], centre[1, 0], centre[0, 1])
            results = (
                centre[0, 0], *flow, total[0, 0], centre[2, 0], centre[0, 2],
                difference[1, 0], difference[0, 1], centre[1, 1],
            )
            for f, value in enumerate(results):
                new[f, z, rows] = value
            for c in range(3):
                start = (c * DEPTH + inner + BZ) * PITCH
                velocity[pl.ds(start + y, CHUNK)] = flow[c]
                if step == 0:
                    velocity[pl.ds(start + SIDE, BXY)] = flow[c]

        @pl.when(z >= 2)
        def _():
            pltpu.make_async_copy(new.at[:, z], out_hbm.at[:, z - 2], out_sem.at[z - 2]).start()

        return carry

    lax.fori_loop(0, PLANES + 2, stream_plane, 0)

    if not last:
        send_planes = [
            pltpu.make_async_copy(new.at[:, PLANES + 1], sendup_hbm.at[pl.ds(0, FIELDS)], send_sem.at[0]),
            pltpu.make_async_copy(new.at[:, 2], senddown_hbm.at[pl.ds(0, FIELDS)], send_sem.at[1]),
        ]
        for copy in send_planes:
            copy.start()

    across = functools.partial(
        lax.dot_general, dimension_numbers=(((1,), (1,)), ((), ())), preferred_element_type=F32
    )

    def sample_box(slot, carry):
        @pl.when(jnp.logical_and(slots_ref[slot * 3] > -BZ, slots_ref[slot * 3] < PLANES))
        def _():
            above, spots, starts, rows = box_parts(slot)
            cells = jnp.concatenate(
                [
                    jnp.concatenate([velocity[pl.ds(start + i, 8, stride=PITCH)] for i in range(8)], axis=1)
                    for start in starts
                ],
                axis=0,
            )
            found = across(jnp.concatenate(split(cells), axis=0), spots)
            plane = lax.broadcasted_iota(jnp.int32, (8, SIDE), 0) + above
            ours = jnp.logical_and(plane >= 0, plane < PLANES)
            for n, start in enumerate(rows):
                value = found[n * 8 : n * 8 + 8] + found[48 + n * 8 : 56 + n * 8]
                sampled[pl.ds(start, 8, stride=BOXED)] = jnp.where(ours, value, 0.0)

        return carry

    lax.fori_loop(0, BLOCKS * OWNED, sample_box, 0)

    part_high, part_low = split(
        jnp.concatenate([sampled[chunk_row(n) : chunk_row(n) + ROWS] for n in range(16)], axis=1)
    )
    main = across(jnp.concatenate([part_high, part_low], axis=0), high_ref[...])
    partial = main[:ROWS] + (main[ROWS:] + across(part_high, low_ref[...]))

    newsum_ref[...] = partial if first else sum_ref[...] + partial
    if not last:
        newstate_ref[...] = state[...] + MOBILITY * partial
        for part in range(3):
            lanes = slice(part * 128, part * 128 + 128)
            for ref, start, owners in ((tail_up, 1, 3), (tail_down, 0, 4)):
                for owner in range(owners):
                    block, row = place(owner * 3 + part)
                    source = (start + owner) * GROUP
                    ref[block, row : row + GROUP] = partial[source : source + GROUP, lanes]
        send_tails = [
            pltpu.make_async_copy(tail_up.at[pl.ds(0, 2)], sendup_hbm.at[pl.ds(FIELDS, 2)], send_sem.at[2]),
            pltpu.make_async_copy(tail_down.at[pl.ds(0, 3)], senddown_hbm.at[pl.ds(FIELDS, 3)], send_sem.at[3]),
        ]
        for copy in send_tails:
            copy.start()
        for copy in send_planes + send_tails:
            copy.wait()
    for z in range(PLANES):
        pltpu.make_async_copy(new.at[:, z + 2], out_hbm.at[:, z], out_sem.at[z]).wait()


def advance(first, last, slots, high, low, moments, up, down, *rest):
    square = (SIDE, SIDE)
    out_shape = [
        jax.ShapeDtypeStruct((FIELDS, PLANES) + square, F32),
        jax.ShapeDtypeStruct((ROWS, LANES), F32),
    ]
    out_specs = [ANY, VMEM]
    if not last:
        out_shape += [
            jax.ShapeDtypeStruct((ROWS, LANES), F32),
            jax.ShapeDtypeStruct((FIELDS + 2,) + square, F32),
            jax.ShapeDtypeStruct((FIELDS + 3,) + square, F32),
        ]
        out_specs += [VMEM, ANY, ANY]
    scratch = [
        pltpu.VMEM((FIELDS, PLANES + 2) + square, F32),
        pltpu.VMEM((FIELDS, PLANES + 2) + square, F32),
        pltpu.VMEM((3 * DEPTH * PITCH, SIDE), F32),
        pltpu.VMEM((3 * DEPTH * PITCH, SIDE), F32),
        pltpu.VMEM((CELLS // 128 * BOXED, 128), F32),
        pltpu.VMEM((CELLS // 128 * BOXED, 128), F32),
        pltpu.VMEM((3,) + square, F32),
        pltpu.VMEM((3,) + square, F32),
        pltpu.VMEM((15, PADDED, SIDE), F32),
        pltpu.VMEM((6,) + square, F32),
        pltpu.VMEM((2, 6) + square, F32),
        pltpu.VMEM((6,) + square, F32),
        pltpu.VMEM((ROWS, LANES), F32),
        pltpu.SemaphoreType.DMA((PLANES + 2,)),
        pltpu.SemaphoreType.DMA((2,)),
        pltpu.SemaphoreType.DMA((PLANES,)),
        pltpu.SemaphoreType.DMA((4,)),
    ]
    return pl.pallas_call(
        functools.partial(step_kernel, first, last),
        out_shape=out_shape,
        in_specs=[SMEM, VMEM, VMEM, ANY, ANY, ANY] + [VMEM] * len(rest),
        out_specs=out_specs,
        scratch_shapes=scratch,
        compiler_params=pltpu.CompilerParams(vmem_limit_bytes=48 * 2**20),
        cost_estimate=pl.CostEstimate(
            flops=4 * 10**8, bytes_accessed=16 * 2**20, transcendentals=0
        ),
        name="first_step" if first else "last_step" if last else "step",
    )(slots, high, low, moments, up, down, *rest)


def per_device(moments, shapes, anchors, synthesis, spreading):
    devices = lax.axis_size("gz")
    total_planes = PLANES * devices
    small = jnp.concatenate(
        [
            shapes.reshape(GROUP, COEFS),
            jnp.zeros((GROUP, ANCHOR_LANE - COEFS), F32),
            anchors.astype(F32).reshape(GROUP, 1),
            jnp.zeros((GROUP, LANES - ANCHOR_LANE - 1), F32),
        ],
        axis=1,
    )
    send_up, send_down = pack(moments, small)
    below2, above2 = shifted(small, 2), shifted(small, -2)
    up, down = shifted(send_up, 1), shifted(send_down, -1)
    high, low = couple(jnp.pad(synthesis, ((0, 0), (0, LANES - COEFS))), spreading)

    block, row = place(2)
    edge = ANCHOR_LANE - 256
    places = jnp.concatenate(
        [
            below2[:, ANCHOR_LANE],
            up[FIELDS + block, row : row + GROUP, edge],
            small[:, ANCHOR_LANE],
            down[FIELDS + block, row : row + GROUP, edge],
            above2[:, ANCHOR_LANE],
        ]
    ).astype(jnp.int32)
    half = total_planes // 2
    local = (places - PLANES * lax.axis_index("gz") + half) % total_planes - half
    slots = jnp.where(jnp.arange(ROWS, dtype=jnp.int32) % 3 == 0, local, places)

    rest = (small, below2, above2)
    for step in range(STEPS):
        last = step == STEPS - 1
        results = advance(step == 0, last, slots, high, low, moments, up, down, *rest)
        moments, sums = results[:2]
        if not last:
            state, send_up, send_down = results[2:]
            up, down = shifted(send_up, 1), shifted(send_down, -1)
            rest = (state, sums)

    group = [sums[i * GROUP : (i + 1) * GROUP] for i in range(BLOCKS)]
    change = group[2] + shifted(group[3], 1) + shifted(group[1], -1) + shifted(group[0], -2)
    change = change[:, :COEFS].reshape(OWNED, 3, COEFS)
    return (moments, shapes + MOBILITY * change)


def solution(mesh):
    return jax.shard_map(
        per_device,
        mesh=mesh,
        in_specs=(P(None, "gz", None, None), P("gz", None, None), P("gz", None), P(), P()),
        out_specs=(P(None, "gz", None, None), P("gz", None, None)),
        check_vma=False,
    )
```

profile of v0, /device:TPU:0, one launch (start us, length us, event | category | flops | bytes accessed | tf_op | source)
XLA Modules:
  0.0 149.0 jit_solution(8683758238619301388)
XLA Ops:
  0.7 0.1 pad.8.clone
  0.8 0.7 convert_element_type.8
  1.5 0.1 copy.14
  1.6 0.8 copy.13
  2.4 0.7 maximum_maximum_fusion.small_ref.refs_6_
  3.1 2.5 %pack.1 = (f32[11,128,128]{2,1,0:T(8,128)}, f32[11,128,128]{2,1,0:T(8,128)}) custom-call(f32[10,8,128,128]{3,2,1,0:T(8,128)} %refs_3_.1, f32[10,8,128,128]{3,2,1,0:T(8,128)} %refs_3_.1, f32[24,384]{1,0:T(8,128)} %maximum_maximum_fusion.small_ref.refs_6_), custom_call_target="tpu_custom_call" | custom-call | tf_op jit(solution)/shard_map/pack/pallas_call | solution.py:103
  5.7 8.2 %collective-permute-start.2 = (f32[11,128,128]{2,1,0:T(8,128)}, f32[11,128,128]{2,1,0:T(8,128)S(1)}, u32[]{:S(2)}, u32[]{:S(2)}) collective-permute-start(f32[11,128,128]{2,1,0:T(8,128)} %get-tuple-element.19), channel_id=1, source_target_pairs={{1,0},{2,1},{3,2},{4,3},{5,4},{6,5},{7,6},{8,7},{9,8},{10,9},{11,1... | collective-permute-start | bytes 2162696 | tf_op jit(solution)/shard_map/ppermute | solution.py:45
  13.9 2.3 %collective-permute-start.3 = (f32[24,384]{1,0:T(8,128)S(1)}, f32[24,384]{1,0:T(8,128)S(1)}, u32[]{:S(2)}, u32[]{:S(2)}) collective-permute-start(f32[24,384]{1,0:T(8,128)S(1)} %copy-done.3), channel_id=1, source_target_pairs={{2,0},{3,1},{4,2},{5,3},{6,4},{7,5},{8,6},{9,7},{10,8},{11,9},{12,... | collective-permute-start | bytes 110600 | tf_op jit(solution)/shard_map/ppermute | solution.py:45
  16.2 0.3 copy.17
  16.5 0.9 pad.4.synthesis_ref
  17.4 6.5 %couple.1 = (bf16[384,2048]{1,0:T(8,128)(2,1)}, bf16[384,2048]{1,0:T(8,128)(2,1)}) custom-call(f32[512,384]{1,0:T(8,128)} %pad.4.synthesis_ref, f32[512,2048]{1,0:T(8,128)} %spreading_ref.1), custom_call_target="tpu_custom_call" | custom-call | flops 2415919104 | bytes 8388608 | tf_op jit(solution)/shard_map/couple/pallas_call | solution.py:76
  23.9 0.1 squeeze_reshape.3
  24.0 0.2 slice_reduce_fusion
  24.1 1.4 collective-permute-done.refs_7_
  25.6 0.2 slice_reduce_fusion.3
  25.8 0.2 slice_reduce_fusion.2
  26.0 0.2 slice_reduce_fusion.1
  26.2 0.1 concatenate.7
  26.3 1.4 copy-done
  27.7 22.4 %first_step.1 = (f32[10,8,128,128]{3,2,1,0:T(8,128)}, f32[120,384]{1,0:T(8,128)S(1)}, f32[120,384]{1,0:T(8,128)S(1)}, f32[12,128,128]{2,1,0:T(8,128)S(1)}, f32[13,128,128]{2,1,0:T(8,128)S(1)}) custom-call(s32[120]{0:T(128)S(1)} %compare_select_fusion.2.refs_0_, bf16[384,2048]{1,0:T(8,128)(2,1)S(1)} %copy-done, bf16[384,2048]{1,0:T(8,128)(2,1)} %get-tuple-element.21.refs_2_, ...), custom_call_target="tpu_custom_call" | custom-call | flops 400000000 | bytes 16777216 | tf_op jit(solution)/shard_map/first_step/pallas_call | solution.py:468
  50.1 6.5 %collective-permute-start.5 = (f32[13,128,128]{2,1,0:T(8,128)S(1)}, f32[13,128,128]{2,1,0:T(8,128)S(1)}, u32[]{:S(2)}, u32[]{:S(2)}) collective-permute-start(f32[13,128,128]{2,1,0:T(8,128)S(1)} %get-tuple-element.24), channel_id=1, source_target_pairs={{1,0},{2,1},{3,2},{4,3},{5,4},{6,5},{7,6},{8,7},{9,8},{10,9},{11,1... | collective-permute-start | bytes 2555912 | tf_op jit(solution)/shard_map/ppermute | solution.py:45
  56.7 16.8 %collective-permute-done.4.refs_4_ = f32[12,128,128]{2,1,0:T(8,128)S(1)} collective-permute-done((f32[12,128,128]{2,1,0:T(8,128)S(1)}, f32[12,128,128]{2,1,0:T(8,128)S(1)}, u32[]{:S(2)}, u32[]{:S(2)}) %collective-permute-start.4) | collective-permute-done | bytes 786464 | tf_op jit(solution)/shard_map/ppermute | solution.py:45
  73.5 22.6 %step.1 = (f32[10,8,128,128]{3,2,1,0:T(8,128)}, f32[120,384]{1,0:T(8,128)S(1)}, f32[120,384]{1,0:T(8,128)S(1)}, f32[12,128,128]{2,1,0:T(8,128)S(1)}, f32[13,128,128]{2,1,0:T(8,128)S(1)}) custom-call(s32[120]{0:T(128)S(1)} %compare_select_fusion.2.refs_0_, bf16[384,2048]{1,0:T(8,128)(2,1)S(1)} %copy-done.1, bf16[384,2048]{1,0:T(8,128)(2,1)} %get-tuple-element.21.refs_2_, ...), custom_call_target="tpu_custom_call" | custom-call | flops 400000000 | bytes 16777216 | tf_op jit(solution)/shard_map/step/pallas_call | solution.py:468
  96.1 2.6 %collective-permute-start.7 = (f32[13,128,128]{2,1,0:T(8,128)S(1)}, f32[13,128,128]{2,1,0:T(8,128)S(1)}, u32[]{:S(2)}, u32[]{:S(2)}) collective-permute-start(f32[13,128,128]{2,1,0:T(8,128)S(1)} %get-tuple-element.29), channel_id=1, source_target_pairs={{1,0},{2,1},{3,2},{4,3},{5,4},{6,5},{7,6},{8,7},{9,8},{10,9},{11,1... | collective-permute-start | bytes 2555912 | tf_op jit(solution)/shard_map/ppermute | solution.py:45
  98.8 16.8 %collective-permute-done.6.refs_4_ = f32[12,128,128]{2,1,0:T(8,128)S(1)} collective-permute-done((f32[12,128,128]{2,1,0:T(8,128)S(1)}, f32[12,128,128]{2,1,0:T(8,128)S(1)}, u32[]{:S(2)}, u32[]{:S(2)}) %collective-permute-start.6) | collective-permute-done | bytes 786464 | tf_op jit(solution)/shard_map/ppermute | solution.py:45
  115.6 21.2 %last_step.1 = (f32[10,8,128,128]{3,2,1,0:T(8,128)}, f32[120,384]{1,0:T(8,128)S(1)}) custom-call(s32[120]{0:T(128)S(1)} %compare_select_fusion.2.refs_0_, bf16[384,2048]{1,0:T(8,128)(2,1)S(1)} %copy-done.1, bf16[384,2048]{1,0:T(8,128)(2,1)S(1)} %copy-done.2, f32[10,8,128,128]{3,2,1,0:T(8,128)} %get-tuple-element.27.refs_3_, ...), custom_call_target="tpu_custom_call" | custom-call | flops 400000000 | bytes 16777216 | tf_op jit(solution)/shard_map/last_step/pallas_call | solution.py:468
  136.8 0.1 collective-permute-start.10
  136.9 2.6 %collective-permute-start.9 = (f32[24,384]{1,0:T(8,128)S(1)}, f32[24,384]{1,0:T(8,128)S(1)}, u32[]{:S(2)}, u32[]{:S(2)}) collective-permute-start(f32[24,384]{1,0:T(8,128)S(1)} %get-tuple-element.38), channel_id=1, source_target_pairs={{1,0},{2,1},{3,2},{4,3},{5,4},{6,5},{7,6},{8,7},{9,8},{10,9},{11,1... | collective-permute-start | bytes 110600 | tf_op jit(solution)/shard_map/ppermute | solution.py:45
  139.6 1.3 collective-permute-done.10
  140.8 0.3 collective-permute-done.9
  141.2 7.2 %collective-permute-done.8 = f32[24,384]{1,0:T(8,128)S(1)} collective-permute-done((f32[24,384]{1,0:T(8,128)S(1)}, f32[24,384]{1,0:T(8,128)S(1)}, u32[]{:S(2)}, u32[]{:S(2)}) %collective-permute-start.8) | collective-permute-done | bytes 36896 | tf_op jit(solution)/shard_map/ppermute | solution.py:45
  148.4 0.6 copy.19
  (31 shorter events, 0.3 us)
Async XLA Ops:
  3.1 10.8 %copy-start.3 = (f32[24,384]{1,0:T(8,128)S(1)}, f32[24,384]{1,0:T(8,128)}, u32[]{:S(2)}) copy-start(f32[24,384]{1,0:T(8,128)} %maximum_maximum_fusion.small_ref.refs_6_) | copy-start | bytes 110596
  3.1 13.1 %copy-start.4 = (f32[512,289]{0,1:T(8,128)S(1)}, f32[512,289]{0,1:T(8,128)}, u32[]{:S(2)}) copy-start(f32[512,289]{0,1:T(8,128)} %param.8) | copy-start | bytes 1775620
  5.7 20.1 %collective-permute-start.1 = (f32[11,128,128]{2,1,0:T(8,128)}, f32[11,128,128]{2,1,0:T(8,128)S(1)}, u32[]{:S(2)}, u32[]{:S(2)}) collective-permute-start(f32[11,128,128]{2,1,0:T(8,128)} %get-tuple-element.18), channel_id=1, source_target_pairs={{127,0},{0,1},{1,2},{2,3},{3,4},{4,5},{5,6},{6,7},{7,8},{8,9},{9,1... | collective-permute-start | bytes 2162696 | tf_op jit(solution)/shard_map/ppermute | solution.py:45
  5.7 20.3 %collective-permute-start.2 = (f32[11,128,128]{2,1,0:T(8,128)}, f32[11,128,128]{2,1,0:T(8,128)S(1)}, u32[]{:S(2)}, u32[]{:S(2)}) collective-permute-start(f32[11,128,128]{2,1,0:T(8,128)} %get-tuple-element.19), channel_id=1, source_target_pairs={{1,0},{2,1},{3,2},{4,3},{5,4},{6,5},{7,6},{8,7},{9,8},{10,9},{11,1... | collective-permute-start | bytes 2162696 | tf_op jit(solution)/shard_map/ppermute | solution.py:45
  13.9 10.1 %collective-permute-start.3 = (f32[24,384]{1,0:T(8,128)S(1)}, f32[24,384]{1,0:T(8,128)S(1)}, u32[]{:S(2)}, u32[]{:S(2)}) collective-permute-start(f32[24,384]{1,0:T(8,128)S(1)} %copy-done.3), channel_id=1, source_target_pairs={{2,0},{3,1},{4,2},{5,3},{6,4},{7,5},{8,6},{9,7},{10,8},{11,9},{12,... | collective-permute-start | bytes 110600 | tf_op jit(solution)/shard_map/ppermute | solution.py:45
  16.2 9.4 %collective-permute-start = (f32[24,384]{1,0:T(8,128)S(1)}, f32[24,384]{1,0:T(8,128)S(1)}, u32[]{:S(2)}, u32[]{:S(2)}) collective-permute-start(f32[24,384]{1,0:T(8,128)S(1)} %copy-done.3), channel_id=1, source_target_pairs={{126,0},{127,1},{0,2},{1,3},{2,4},{3,5},{4,6},{5,7},{6,8},{7,9},{8... | collective-permute-start | bytes 110600 | tf_op jit(solution)/shard_map/ppermute | solution.py:45
  26.3 1.4 copy-start
  27.7 45.8 %copy-start.1 = (bf16[384,2048]{1,0:T(8,128)(2,1)S(1)}, bf16[384,2048]{1,0:T(8,128)(2,1)}, u32[]{:S(2)}) copy-start(bf16[384,2048]{1,0:T(8,128)(2,1)} %get-tuple-element.20.refs_1_) | copy-start | bytes 4718596
  50.1 65.5 %copy-start.2 = (bf16[384,2048]{1,0:T(8,128)(2,1)S(1)}, bf16[384,2048]{1,0:T(8,128)(2,1)}, u32[]{:S(2)}) copy-start(bf16[384,2048]{1,0:T(8,128)(2,1)} %get-tuple-element.21.refs_2_) | copy-start | bytes 4718596
  50.1 23.4 %collective-permute-start.5 = (f32[13,128,128]{2,1,0:T(8,128)S(1)}, f32[13,128,128]{2,1,0:T(8,128)S(1)}, u32[]{:S(2)}, u32[]{:S(2)}) collective-permute-start(f32[13,128,128]{2,1,0:T(8,128)S(1)} %get-tuple-element.24), channel_id=1, source_target_pairs={{1,0},{2,1},{3,2},{4,3},{5,4},{6,5},{7,6},{8,7},{9,8},{10,9},{11,1... | collective-permute-start | bytes 2555912 | tf_op jit(solution)/shard_map/ppermute | solution.py:45
  56.7 16.8 %collective-permute-start.4 = (f32[12,128,128]{2,1,0:T(8,128)S(1)}, f32[12,128,128]{2,1,0:T(8,128)S(1)}, u32[]{:S(2)}, u32[]{:S(2)}) collective-permute-start(f32[12,128,128]{2,1,0:T(8,128)S(1)} %get-tuple-element.23), channel_id=1, source_target_pairs={{127,0},{0,1},{1,2},{2,3},{3,4},{4,5},{5,6},{6,7},{7,8},{8,9},{9,1... | collective-permute-start | bytes 2359304 | tf_op jit(solution)/shard_map/ppermute | solution.py:45
  96.1 19.5 %collective-permute-start.7 = (f32[13,128,128]{2,1,0:T(8,128)S(1)}, f32[13,128,128]{2,1,0:T(8,128)S(1)}, u32[]{:S(2)}, u32[]{:S(2)}) collective-permute-start(f32[13,128,128]{2,1,0:T(8,128)S(1)} %get-tuple-element.29), channel_id=1, source_target_pairs={{1,0},{2,1},{3,2},{4,3},{5,4},{6,5},{7,6},{8,7},{9,8},{10,9},{11,1... | collective-permute-start | bytes 2555912 | tf_op jit(solution)/shard_map/ppermute | solution.py:45
  98.8 16.8 %collective-permute-start.6 = (f32[12,128,128]{2,1,0:T(8,128)S(1)}, f32[12,128,128]{2,1,0:T(8,128)S(1)}, u32[]{:S(2)}, u32[]{:S(2)}) collective-permute-start(f32[12,128,128]{2,1,0:T(8,128)S(1)} %get-tuple-element.28), channel_id=1, source_target_pairs={{127,0},{0,1},{1,2},{2,3},{3,4},{4,5},{5,6},{6,7},{7,8},{8,9},{9,1... | collective-permute-start | bytes 2359304 | tf_op jit(solution)/shard_map/ppermute | solution.py:45
  115.6 32.8 %copy-start.5 = (f32[8,3,289]{2,0,1:T(8,128)S(1)}, f32[8,3,289]{2,0,1:T(8,128)}, u32[]{:S(2)}) copy-start(f32[8,3,289]{2,0,1:T(8,128)} %param.6) | copy-start | bytes 83236
  136.8 4.0 %collective-permute-start.10 = (f32[24,384]{1,0:T(8,128)S(1)}, f32[24,384]{1,0:T(8,128)S(1)}, u32[]{:S(2)}, u32[]{:S(2)}) collective-permute-start(f32[24,384]{1,0:T(8,128)S(1)} %get-tuple-element.37), channel_id=1, source_target_pairs={{2,0},{3,1},{4,2},{5,3},{6,4},{7,5},{8,6},{9,7},{10,8},{11,9},{12,... | collective-permute-start | bytes 110600 | tf_op jit(solution)/shard_map/ppermute | solution.py:45
  136.9 4.3 %collective-permute-start.9 = (f32[24,384]{1,0:T(8,128)S(1)}, f32[24,384]{1,0:T(8,128)S(1)}, u32[]{:S(2)}, u32[]{:S(2)}) collective-permute-start(f32[24,384]{1,0:T(8,128)S(1)} %get-tuple-element.38), channel_id=1, source_target_pairs={{1,0},{2,1},{3,2},{4,3},{5,4},{6,5},{7,6},{8,7},{9,8},{10,9},{11,1... | collective-permute-start | bytes 110600 | tf_op jit(solution)/shard_map/ppermute | solution.py:45
  139.5 8.8 %collective-permute-start.8 = (f32[24,384]{1,0:T(8,128)S(1)}, f32[24,384]{1,0:T(8,128)S(1)}, u32[]{:S(2)}, u32[]{:S(2)}) collective-permute-start(f32[24,384]{1,0:T(8,128)S(1)} %get-tuple-element.39), channel_id=1, source_target_pairs={{127,0},{0,1},{1,2},{2,3},{3,4},{4,5},{5,6},{6,7},{7,8},{8,9},{9,1... | collective-permute-start | bytes 110600 | tf_op jit(solution)/shard_map/ppermute | solution.py:45
where the time goes:
time: 148 us; the launch traced here: 149 us
  Pallas kernels  75.2 us (51%)
  waiting for transfers between devices  43.9 us (30%)
  starting transfers between devices  22.5 us (15%)
  local copies, waits for them, and re-layouts  5.27 us (4%)
    pallas_call x3, Pallas kernels, advance(): pl.pallas_call(functools.partial(step_kernel, first, last), out_shape=out...  66.2 us
    ppermute x11, waiting for transfers between devices, shifted(): lax.ppermute(block, 'gz', [((i - distance) % devices, i) for i in range(d...  43.9 us
    ppermute x11, starting transfers between devices, shifted(): lax.ppermute(block, 'gz', [((i - distance) % devices, i) for i in range(d...  22.5 us
    pallas_call x1, Pallas kernels, couple(): pl.pallas_call(couple_kernel, out_shape=(shape, shape), grid=(CELLS // wi...  6.47 us
    unnamed x15, local copies, waits for them, and re-layouts  3.09 us
  transfers between devices with their start and end apart: 11, of which 6 were waited for; matrix products, arithmetic and copies ran while one was open for 1% of the time, Pallas kernels for 4%

commit v1 on v0

v1 whole, which is shorter than its diff:
```python
import functools

import jax
import jax.numpy as jnp
from jax import lax
from jax.experimental import pallas as pl
from jax.experimental.pallas import tpu as pltpu
from jax.sharding import PartitionSpec as P


LMAX = 16
BZ = 8
BXY = 16
STEPS = 3
STIFF_SCALE = 0.002
MOBILITY = 0.5

PLANES = 8
SIDE = 128
OWNED = 8
COEFS = 289
SLOTS = 40
LANES = 384
KEPT = 304
CELLS = 2048
POINTS = 512
GROUP = OWNED * 3
BLOCKS = 5
ROWS = GROUP * BLOCKS
ANCHOR_LANE = 300
FIELDS = 10
SENT = 9 * SIDE
NARROW = COEFS - 256
STEP_LANES = 40
PADDED = 144
PITCH = 145
DEPTH = PLANES + 2 * BZ + 1
BOXED = ROWS + 1
CHUNK = 16
JK = ((0, 0), (1, 0), (2, 0), (0, 1), (1, 1), (0, 2))

VMEM = pl.BlockSpec(memory_space=pltpu.VMEM)
SMEM = pl.BlockSpec(memory_space=pltpu.SMEM)
HBM = pl.BlockSpec(memory_space=pltpu.HBM)
F32 = jnp.float32
BF16 = jnp.bfloat16


def shifted(block, distance):
    devices = lax.axis_size("gz")
    return lax.ppermute(block, "gz", [((i - distance) % devices, i) for i in range(devices)])


def split(value):
    high = value.astype(BF16)
    return high, (value - high.astype(F32)).astype(BF16)


def tail_rows(owner, part, owners):
    if part < 2:
        group, lane = owner * 2 + part, 0
    else:
        group, lane = owners * 2 + owner // 3, STEP_LANES * (owner % 3)
    start = SENT + group * GROUP
    return slice(start, start + GROUP), lane


def message_rows(owners):
    return SENT + (owners * 2 + (owners + 2) // 3) * GROUP


def read_tail(ref, owner, part, owners):
    rows, lane = tail_rows(owner, part, owners)
    value = ref[rows]
    if part == 2:
        if lane:
            value = pltpu.roll(value, 128 - lane, 1)
        lanes = lax.broadcasted_iota(jnp.int32, value.shape, 1)
        value = jnp.where(lanes < NARROW, value, 0.0)
    return value


def write_tail(ref, values, width):
    owners = values
    for owner in range(owners):
        for part in range(2):
            ref[tail_rows(owner, part, owners)[0]] = width(owner, part)
    for first in range(0, owners, 3):
        packed = width(first, 2)
        for owner in range(first + 1, min(first + 3, owners)):
            packed = packed + pltpu.roll(width(owner, 2), STEP_LANES * (owner - first), 1)
        ref[tail_rows(first, 2, owners)[0]] = packed


def write_plane(ref, field):
    trace = field(4)
    values = [field(0) - 0.6 * trace, field(1), field(2), field(3)]
    values += [field(5) - 0.2 * trace, field(6) - 0.2 * trace, field(7), field(8), field(9)]
    for n, value in enumerate(values):
        ref[n * SIDE : n * SIDE + SIDE] = value


def slot_row(slot):
    return slot + (slot // OWNED) * (2 * OWNED)


def chunk_row(n):
    return (n % 2 * 8 + n // 2) * BOXED


def couple_kernel(synthesis_ref, spreading_ref, high_ref, low_ref):
    width = 512
    turned = jnp.concatenate(split(synthesis_ref[...].T[0:KEPT]), axis=0)
    for ref in (high_ref, low_ref):
        ref[KEPT:] = jnp.zeros((LANES - KEPT, CELLS), BF16)
    for first in range(0, CELLS, width):
        lanes = slice(first, first + width)
        w_high, w_low = split(spreading_ref[:, lanes])
        main = jnp.dot(turned, w_high, preferred_element_type=F32)
        rest = jnp.dot(turned[0:KEPT], w_low, preferred_element_type=F32)
        high_ref[0:KEPT, lanes], low_ref[0:KEPT, lanes] = split(main[:KEPT] + (main[KEPT:] + rest))


def couple(synthesis, spreading):
    shape = jax.ShapeDtypeStruct((LANES, CELLS), BF16)
    return pl.pallas_call(
        couple_kernel,
        out_shape=(shape, shape),
        in_specs=[VMEM, VMEM],
        out_specs=[VMEM, VMEM],
        compiler_params=pltpu.CompilerParams(vmem_limit_bytes=32 * 2**20),
        cost_estimate=pl.CostEstimate(
            flops=6 * LANES * POINTS * CELLS, bytes_accessed=8 * 2**20, transcendentals=0
        ),
        name="couple",
    )(synthesis, spreading)


def pack_kernel(anchors_ref, moments_hbm, shapes_ref, small_ref, up_ref, down_ref, planes, sem):
    copies = [
        pltpu.make_async_copy(moments_hbm.at[:, z], planes.at[n], sem.at[n])
        for n, z in enumerate((PLANES - 1, 0))
    ]
    for copy in copies:
        copy.start()
    small_ref[...] = jnp.zeros_like(small_ref)
    for c in range(3):
        small_ref[c * OWNED : c * OWNED + OWNED, 0:COEFS] = shapes_ref[c]
    part = small_ref[:, 256:LANES]
    row = lax.broadcasted_iota(jnp.int32, part.shape, 0)
    anchor = jnp.zeros(part.shape, jnp.int32)
    for n in range(GROUP):
        anchor = jnp.where(row == n, anchors_ref[n // OWNED, n % OWNED], anchor)
    lane = lax.broadcasted_iota(jnp.int32, part.shape, 1)
    part = jnp.where(lane == ANCHOR_LANE - 256, anchor.astype(F32), part)
    small_ref[:, 256:LANES] = part
    for ref in (up_ref, down_ref):
        write_tail(ref, 1, lambda owner, p: small_ref[:, p * 128 : p * 128 + 128])
    for n, ref in enumerate((up_ref, down_ref)):
        copies[n].wait()
        write_plane(ref, lambda f, n=n: planes[n, f])


def pack(moments, shapes, anchors):
    shape = jax.ShapeDtypeStruct((message_rows(1), SIDE), F32)
    return pl.pallas_call(
        pack_kernel,
        out_shape=(jax.ShapeDtypeStruct((GROUP, LANES), F32), shape, shape),
        in_specs=[SMEM, HBM, VMEM],
        out_specs=[VMEM, VMEM, VMEM],
        scratch_shapes=[pltpu.VMEM((2, FIELDS, SIDE, SIDE), F32), pltpu.SemaphoreType.DMA((2,))],
        compiler_params=pltpu.CompilerParams(vmem_limit_bytes=60 * 2**20),
        name="pack",
    )(anchors, moments, shapes)


def spread_x(zero, one, two):
    plus = zero if two is None else zero + two
    minus = plus
    if one is not None:
        plus, minus = plus + one, plus - one
    plus = pltpu.roll(plus, 1, 1)
    minus = pltpu.roll(minus, SIDE - 1, 1)
    both = plus + minus
    return (4.0 * zero + both, plus - minus, both)


def collide_rows(m, force):
    unit = 1.0 / 216.0
    rho = m[0]
    u = [m[1 + a] + 0.5 * force[a] for a in range(3)]
    t = [0.625 * u[a] + 0.375 * force[a] for a in range(3)]
    v = [(9.0 * unit) * u[a] for a in range(3)]
    line = [(3.0 * unit) * (m[1 + a] + force[a]) for a in range(3)]
    shared = (0.375 * unit) * rho
    square = [shared - (1.125 * unit) * m[4 + a] + v[a] * t[a] for a in range(3)]
    cross = [
        v[a] * t[b] + v[b] * t[a] - (2.25 * unit) * m[7 + n]
        for n, (a, b) in enumerate(((0, 1), (0, 2), (1, 2)))
    ]
    cell = unit * rho - (1.0 / 3.0) * (square[0] + square[1] + square[2])
    return cell, line, square, cross


def step_kernel(first, last, *refs):
    refs = list(refs)

    def take(count):
        taken = refs[:count]
        del refs[:count]
        return taken

    slots_ref, high_ref, low_ref, moments_hbm, up_ref, down_ref = take(6)
    if first:
        own_ref, below_ref, above_ref = take(3)
    else:
        state_ref, sum_ref, order_ref = take(3)
    out_hbm, newsum_ref = take(2)
    if not last:
        newstate_ref, sendup_ref, senddown_ref = take(3)
    if first:
        (order_ref,) = take(1)
    (
        old, new, velocity, force, boxes, sampled,
        shifts, stills, ring, middle, state,
        in_sem, out_sem,
    ) = refs

    for z in range(PLANES):
        pltpu.make_async_copy(moments_hbm.at[:, z], old.at[:, z + 1], in_sem.at[z]).start()

    if first:

        def scan(slot, carry):
            count, spare = carry
            above = slots_ref[slot_row(slot)]
            near = jnp.logical_and(above >= -BZ, above <= PLANES)

            @pl.when(near)
            def _():
                order_ref[count] = slot

            return count + near.astype(jnp.int32), jnp.where(near, spare, slot)

        count, spare = lax.fori_loop(0, SLOTS, scan, (jnp.int32(0), jnp.int32(0)))
        order_ref[count] = spare
        order_ref[SLOTS + 1] = (count + 1) // 2
    pairs = order_ref[SLOTS + 1]

    for c in range(3):
        start = (c * DEPTH + BZ - 1) * PITCH
        force[start : start + (PLANES + 2) * PITCH] = jnp.zeros(((PLANES + 2) * PITCH, SIDE), F32)
    sampled[...] = jnp.zeros_like(sampled)
    for ref, edge in ((up_ref, 0), (down_ref, PLANES + 1)):
        for n, f in enumerate((0, 1, 2, 3, 5, 6, 7, 8, 9)):
            old[f, edge] = ref[n * SIDE : n * SIDE + SIDE]
        old[4, edge] = jnp.zeros((SIDE, SIDE), F32)

    for part in range(3):
        lanes = slice(part * 128, part * 128 + 128)
        for owner in range(BLOCKS):
            rows = slice(owner * GROUP, owner * GROUP + GROUP)
            if first:
                if owner % 2 == 1:
                    value = read_tail(up_ref if owner == 1 else down_ref, 0, part, 1)
                else:
                    value = (below_ref, own_ref, above_ref)[owner // 2][:, lanes]
                    if part == 2:
                        lane = lax.broadcasted_iota(jnp.int32, value.shape, 1)
                        value = jnp.where(lane < NARROW, value, 0.0)
            else:
                value = state_ref[rows, lanes]
                if owner < 3:
                    value = value + MOBILITY * read_tail(up_ref, owner, part, 3)
                if owner > 0:
                    value = value + MOBILITY * read_tail(down_ref, owner - 1, part, 4)
            state[rows, lanes] = value

    number = lax.broadcasted_iota(jnp.int32, (1, LANES), 1)
    degree = jnp.zeros((1, LANES), jnp.int32)
    for step in range(1, LMAX + 1):
        degree = degree + (number >= step * step).astype(jnp.int32)
    stiffness = STIFF_SCALE * (degree * (degree + 1) + 2).astype(F32)
    coef_high, coef_low = split(-stiffness * state[...])
    both = jnp.concatenate([coef_high, coef_low], axis=0)
    for part in range(CELLS // 512):
        lanes = slice(part * 512, part * 512 + 512)
        main = jnp.dot(both, high_ref[:, lanes], preferred_element_type=F32)
        rest = jnp.dot(coef_high, low_ref[:, lanes], preferred_element_type=F32)
        whole = main[:ROWS] + (main[ROWS:] + rest)
        for chunk in range(4):
            start = chunk_row(part * 4 + chunk)
            boxes[start : start + ROWS] = whole[:, chunk * 128 : chunk * 128 + 128]

    def box_parts(slot):
        base = slot_row(slot)
        above = slots_ref[base]
        near = jnp.logical_and(above >= -BZ, above <= PLANES)
        above = jnp.where(near, above, PLANES + 1)
        row = slots_ref[base + OWNED]
        column = slots_ref[base + 2 * OWNED]
        lane = lax.broadcasted_iota(jnp.int32, (BXY, SIDE), 1)
        inside = lax.broadcasted_iota(jnp.int32, (BXY, SIDE), 0)
        hit = (((lane - column) & (SIDE - 1)) == inside).astype(F32).astype(BF16)
        none = jnp.zeros((BXY, SIDE), BF16)
        spots = jnp.concatenate(
            [jnp.concatenate([hit if i == n else none for i in range(8)], axis=1) for n in range(8)],
            axis=0,
        )
        starts = [
            (c * DEPTH + above + BZ) * PITCH + row + half * 8 for c in range(3) for half in range(2)
        ]
        rows = [half * 8 * BOXED + base + c * OWNED for c in range(3) for half in range(2)]
        return above, spots, starts, rows

    def place_pair(pair, carry):
        found = []
        for n in range(2):
            _, spots, starts, rows = box_parts(order_ref[pair * 2 + n])
            cells = jnp.concatenate([boxes[pl.ds(start, 8, stride=BOXED)] for start in rows], axis=0)
            placed = jnp.dot(
                jnp.concatenate(split(cells), axis=1),
                jnp.concatenate([spots, spots], axis=0),
                preferred_element_type=F32,
            )
            found.append((starts, placed))
        for starts, placed in found:
            where = [
                (pl.ds(start + i, 8, stride=PITCH), slice(n * 8, n * 8 + 8), slice(i * 128, i * 128 + 128))
                for n, start in enumerate(starts)
                for i in range(8)
            ]
            sums = [force[there] + placed[here, lanes] for there, here, lanes in where]
            for (there, here, lanes), value in zip(where, sums):
                force[there] = value
        return carry

    lax.fori_loop(0, pairs, place_pair, 0)

    def fold(z, carry):
        for c in range(3):
            start = (c * DEPTH + z + BZ - 1) * PITCH
            first = pl.ds(start, BXY)
            force[first] = force[first] + force[pl.ds(start + SIDE, BXY)]
        return carry

    lax.fori_loop(0, PLANES + 2, fold, 0)

    def stream_plane(z, carry):
        @pl.when(jnp.logical_and(z >= 1, z <= PLANES))
        def _():
            pltpu.make_async_copy(moments_hbm.at[:, 0], old.at[:, z], in_sem.at[z - 1]).wait()


        def collide_chunk(step, carry):
            y = pl.multiple_of(step * CHUNK, CHUNK)
            rows = pl.ds(y, CHUNK)
            m = [old[f, z, rows] for f in range(FIELDS)]
            cell, line, square, cross = collide_rows(
                m, [force[pl.ds((c * DEPTH + z + BZ - 1) * PITCH + y, CHUNK)] for c in range(3)]
            )
            even = [
                spread_x(cell, line[2], square[2]),
                spread_x(line[1], cross[2], None),
                spread_x(square[1], None, None),
            ]
            twice = spread_x(square[0], None, None)
            odd = [spread_x(line[0], cross[1], None), spread_x(cross[0], None, None)]
            moved = pl.ds(y + 8, CHUNK)
            for k in range(3):
                ends = even[0][k] + even[2][k]
                shifts[k, moved] = ends + even[1][k]
                shifts[3 + k, moved] = ends - even[1][k]
                shifts[6 + k, moved] = odd[0][k] + odd[1][k]
                shifts[9 + k, moved] = odd[0][k] - odd[1][k]
                shifts[12 + k, moved] = twice[k]
                stills[k, rows] = 4.0 * even[0][k]
                stills[3 + k, rows] = 4.0 * odd[0][k]
            return carry

        lax.fori_loop(0, SIDE // CHUNK, collide_chunk, 0)
        for field in range(15):
            shifts[field, 7:8] = shifts[field, SIDE + 7 : SIDE + 8]
            shifts[field, SIDE + 8 : SIDE + 9] = shifts[field, 8:9]
        parity = z % 2
        inner = jnp.clip(z - 2, 0, PLANES - 1)

        for step in range(SIDE // CHUNK):
            y = step * CHUNK
            rows = slice(y, y + CHUNK)
            after = slice(y + 7, y + 7 + CHUNK)
            before = slice(y + 9, y + 9 + CHUNK)
            even, odd, twice = {}, {}, {}
            for k in range(3):
                for target, plus, minus, still in (
                    (even, k, 3 + k, lambda k=k: stills[k, rows]),
                    (odd, 6 + k, 9 + k, lambda k=k: stills[3 + k, rows]),
                    (twice, 12 + k, 12 + k, lambda k=k: 4.0 * shifts[12 + k, y + 8 : y + 8 + CHUNK]),
                ):
                    up, down = shifts[plus, after], shifts[minus, before]
                    both = up + down
                    target[0, k] = still() + both
                    if k < 2:
                        target[1, k] = up - down
                    if k < 1:
                        target[2, k] = both
            total, difference, centre = {}, {}, {}
            for n, key in enumerate(JK):
                ends = even[key] + twice[key]
                under = ring[parity, n, rows]
                over = ends - odd[key]
                total[key] = under + over
                difference[key] = under - over
                centre[key] = middle[n, rows] + total[key]
                ring[parity, n, rows] = ends + odd[key]
                middle[n, rows] = 4.0 * even[key]
            flow = (difference[0, 0], centre[1, 0], centre[0, 1])
            results = (
                centre[0, 0], *flow, total[0, 0], centre[2, 0], centre[0, 2],
                difference[1, 0], difference[0, 1], centre[1, 1],
            )
            for f, value in enumerate(results):
                new[f, z, rows] = value
            for c in range(3):
                start = (c * DEPTH + inner + BZ) * PITCH
                velocity[pl.ds(start + y, CHUNK)] = flow[c]
                if step == 0:
                    velocity[pl.ds(start + SIDE, BXY)] = flow[c]

        @pl.when(z >= 2)
        def _():
            pltpu.make_async_copy(new.at[:, z], out_hbm.at[:, z - 2], out_sem.at[z - 2]).start()

        return carry

    lax.fori_loop(0, PLANES + 2, stream_plane, 0)

    if not last:
        write_plane(sendup_ref, lambda f: new[f, PLANES + 1])
        write_plane(senddown_ref, lambda f: new[f, 2])

    across = functools.partial(
        lax.dot_general, dimension_numbers=(((1,), (1,)), ((), ())), preferred_element_type=F32
    )

    def sample_pair(pair, carry):
        results = []
        for n in range(2):
            above, spots, starts, rows = box_parts(order_ref[pair * 2 + n])
            cells = jnp.concatenate(
                [
                    jnp.concatenate([velocity[pl.ds(start + i, 8, stride=PITCH)] for i in range(8)], axis=1)
                    for start in starts
                ],
                axis=0,
            )
            results.append((above, rows, across(jnp.concatenate(split(cells), axis=0), spots)))
        for above, rows, found in results:
            plane = lax.broadcasted_iota(jnp.int32, (8, SIDE), 0) + above
            ours = jnp.logical_and(plane >= 0, plane < PLANES)
            for n, start in enumerate(rows):
                value = found[n * 8 : n * 8 + 8] + found[48 + n * 8 : 56 + n * 8]
                sampled[pl.ds(start, 8, stride=BOXED)] = jnp.where(ours, value, 0.0)
        return carry

    lax.fori_loop(0, pairs, sample_pair, 0)

    part_high, part_low = split(
        jnp.concatenate([sampled[chunk_row(n) : chunk_row(n) + ROWS] for n in range(16)], axis=1)
    )
    main = across(jnp.concatenate([part_high, part_low], axis=0), high_ref[...])
    partial = main[:ROWS] + (main[ROWS:] + across(part_high, low_ref[...]))

    newsum_ref[...] = partial if first else sum_ref[...] + partial
    if not last:
        newstate_ref[...] = state[...] + MOBILITY * partial
        for ref, start, owners in ((sendup_ref, GROUP, 3), (senddown_ref, 0, 4)):
            write_tail(
                ref,
                owners,
                lambda owner, part: partial[
                    start + owner * GROUP : start + owner * GROUP + GROUP, part * 128 : part * 128 + 128
                ],
            )
    for z in range(PLANES):
        pltpu.make_async_copy(new.at[:, z + 2], out_hbm.at[:, z], out_sem.at[z]).wait()


def advance(first, last, slots, high, low, moments, up, down, *rest):
    square = (SIDE, SIDE)
    out_shape = [
        jax.ShapeDtypeStruct((FIELDS, PLANES) + square, F32),
        jax.ShapeDtypeStruct((ROWS, LANES), F32),
    ]
    out_specs = [HBM, VMEM]
    if not last:
        out_shape += [
            jax.ShapeDtypeStruct((ROWS, LANES), F32),
            jax.ShapeDtypeStruct((message_rows(3), SIDE), F32),
            jax.ShapeDtypeStruct((message_rows(4), SIDE), F32),
        ]
        out_specs += [VMEM] * 3
    if first:
        out_shape.append(jax.ShapeDtypeStruct((SLOTS + 2,), jnp.int32))
        out_specs.append(SMEM)
    scratch = [
        pltpu.VMEM((FIELDS, PLANES + 2) + square, F32),
        pltpu.VMEM((FIELDS, PLANES + 2) + square, F32),
        pltpu.VMEM((3 * DEPTH * PITCH, SIDE), F32),
        pltpu.VMEM((3 * DEPTH * PITCH, SIDE), F32),
        pltpu.VMEM((CELLS // 128 * BOXED, 128), F32),
        pltpu.VMEM((CELLS // 128 * BOXED, 128), F32),
        pltpu.VMEM((15, PADDED, SIDE), F32),
        pltpu.VMEM((6,) + square, F32),
        pltpu.VMEM((2, 6) + square, F32),
        pltpu.VMEM((6,) + square, F32),
        pltpu.VMEM((ROWS, LANES), F32),
        pltpu.SemaphoreType.DMA((PLANES,)),
        pltpu.SemaphoreType.DMA((PLANES,)),
    ]
    return pl.pallas_call(
        functools.partial(step_kernel, first, last),
        out_shape=out_shape,
        in_specs=[SMEM, VMEM, VMEM, HBM, VMEM, VMEM] + [VMEM] * 2 + [VMEM if first else SMEM],
        out_specs=out_specs,
        scratch_shapes=scratch,
        compiler_params=pltpu.CompilerParams(vmem_limit_bytes=44 * 2**20),
        cost_estimate=pl.CostEstimate(
            flops=4 * 10**8, bytes_accessed=16 * 2**20, transcendentals=0
        ),
        input_output_aliases={} if first else {3: 0},
        name="first_step" if first else "last_step" if last else "step",
    )(slots, high, low, moments, up, down, *rest)


def per_device(moments, shapes, anchors, synthesis, spreading):
    devices = lax.axis_size("gz")
    total_planes = PLANES * devices
    small, send_up, send_down = pack(moments, jnp.transpose(shapes, (1, 0, 2)), anchors.T)
    up = shifted(send_up, 1)
    down = shifted(send_down, -1)
    below2 = shifted(small, 2)
    above2 = shifted(small, -2)
    high, low = couple(jnp.pad(synthesis, ((0, 0), (0, LANES - COEFS))), spreading)

    rows, edge = tail_rows(0, 2, 1)[0], ANCHOR_LANE - 256
    places = jnp.concatenate(
        [
            below2[:, ANCHOR_LANE],
            up[rows, edge],
            small[:, ANCHOR_LANE],
            down[rows, edge],
            above2[:, ANCHOR_LANE],
        ]
    ).astype(jnp.int32)
    half = total_planes // 2
    local = (places - PLANES * lax.axis_index("gz") + half) % total_planes - half
    slots = jnp.where(jnp.arange(ROWS, dtype=jnp.int32) % GROUP < OWNED, local, places)

    rest = (small, below2, above2)
    for step in range(STEPS):
        last = step == STEPS - 1
        results = advance(step == 0, last, slots, high, low, moments, up, down, *rest)
        moments, sums = results[:2]
        if not last:
            state, send_up, send_down = results[2:5]
            if step == 0:
                order = results[5]
            up, down = shifted(send_up, 1), shifted(send_down, -1)
            rest = (state, sums, order)

    group = [sums[i * GROUP : (i + 1) * GROUP] for i in range(BLOCKS)]
    change = group[2] + shifted(group[3], 1) + shifted(group[1], -1) + shifted(group[0], -2)
    change = jnp.transpose(change.reshape(3, OWNED, LANES)[:, :, :COEFS], (1, 0, 2))
    return (moments, shapes + MOBILITY * change)


def solution(mesh):
    return jax.shard_map(
        per_device,
        mesh=mesh,
        in_specs=(P(None, "gz", None, None), P("gz", None, None), P("gz", None), P(), P()),
        out_specs=(P(None, "gz", None, None), P("gz", None, None)),
        check_vma=False,
    )
```

time: 148 us -> 135 us (0.912)
  the two profiles are of different devices: /device:TPU:0 before, /device:TPU:1 now
where the time goes in v1:
time: 135 us
  Pallas kernels  63.5 us (47%)
  starting transfers between devices  41.6 us (31%)
  waiting for transfers between devices  23.1 us (17%)
  local copies, waits for them, and re-layouts  4.92 us (4%)
    pallas_call x3, Pallas kernels, advance(): pl.pallas_call(functools.partial(step_kernel, first, last), out_shape=out...  58.2 us
    ppermute x11, starting transfers between devices, shifted(): lax.ppermute(block, 'gz', [((i - distance) % devices, i) for i in range(d...  41.6 us
    ppermute x11, waiting for transfers between devices, shifted(): lax.ppermute(block, 'gz', [((i - distance) % devices, i) for i in range(d...  23.1 us
    pallas_call x1, Pallas kernels, pack(): pl.pallas_call(pack_kernel, out_shape=(jax.ShapeDtypeStruct((GROUP, LANES...  3.2 us
  transfers between devices with their start and end apart: 11, of which 6 were waited for; matrix products, arithmetic and copies ran while one was open for 1% of the time, Pallas kernels for 2%

profile of v1, /device:TPU:1, one launch (start us, length us, event | category | flops | bytes accessed | tf_op | source)
XLA Modules:
  0.0 134.6 jit_solution(17751007490388032671)
XLA Ops:
  0.6 3.2 %pack.1 = (f32[24,384]{1,0:T(8,128)}, f32[1224,128]{1,0:T(8,128)}, f32[1224,128]{1,0:T(8,128)}) custom-call(s32[3,8]{1,0:T(4,128)} %bitcast.9, f32[10,8,128,128]{3,2,1,0:T(8,128)} %refs_3_.1, f32[3,8,289]{2,1,0:T(8,128)} %bitcast.8), custom_call_target="tpu_custom_call" | custom-call | tf_op jit(solution)/shard_map/pack/pallas_call | solution.py:166
  3.8 3.1 %collective-permute-start.1 = (f32[1224,128]{1,0:T(8,128)}, f32[1224,128]{1,0:T(8,128)}, u32[]{:S(2)}, u32[]{:S(2)}) collective-permute-start(f32[1224,128]{1,0:T(8,128)} %get-tuple-element.21), channel_id=1, source_target_pairs={{127,0},{0,1},{1,2},{2,3},{3,4},{4,5},{5,6},{6,7},{7,8},{8,9},{9,1... | collective-permute-start | bytes 1880072 | tf_op jit(solution)/shard_map/ppermute | solution.py:51
  6.9 6.3 %collective-permute-start.3 = (f32[24,384]{1,0:T(8,128)}, f32[24,384]{1,0:T(8,128)S(1)}, u32[]{:S(2)}, u32[]{:S(2)}) collective-permute-start(f32[24,384]{1,0:T(8,128)} %get-tuple-element.20.refs_6_), channel_id=1, source_target_pairs={{2,0},{3,1},{4,2},{5,3},{6,4},{7,5},{8,6},{9,7},{10,8},{11,9},{12,... | collective-permute-start | bytes 110600 | tf_op jit(solution)/shard_map/ppermute | solution.py:51
  13.2 1.0 collective-permute-start.2
  14.2 0.3 copy.10
  14.5 0.0 copy-start
  14.5 0.1 pad.4.synthesis_ref
  14.5 0.0 copy-start.1
  14.5 2.2 %copy-done.1 = f32[512,2048]{1,0:T(8,128)S(1)} copy-done((f32[512,2048]{1,0:T(8,128)S(1)}, f32[512,2048]{1,0:T(8,128)}, u32[]{:S(2)}) %copy-start.1) | copy-done | bytes 4194328
  16.7 2.2 %couple.1 = (bf16[384,2048]{1,0:T(8,128)(2,1)S(1)}, bf16[384,2048]{1,0:T(8,128)(2,1)S(1)}) custom-call(f32[512,384]{1,0:T(8,128)S(1)} %pad.4.synthesis_ref, f32[512,2048]{1,0:T(8,128)S(1)} %copy-done.1), custom_call_target="tpu_custom_call" | custom-call | flops 2415919104 | bytes 8388608 | tf_op jit(solution)/shard_map/couple/pallas_call | solution.py:126
  18.9 0.2 slice_reduce_fusion.4
  19.1 0.2 slice_reduce_fusion
  19.3 2.4 %collective-permute-done.refs_7_ = f32[24,384]{1,0:T(8,128)S(1)} collective-permute-done((f32[24,384]{1,0:T(8,128)}, f32[24,384]{1,0:T(8,128)S(1)}, u32[]{:S(2)}, u32[]{:S(2)}) %collective-permute-start) | collective-permute-done | bytes 36896 | tf_op jit(solution)/shard_map/ppermute | solution.py:51
  21.7 0.2 slice_reduce_fusion.3
  21.9 0.0 collective-permute-done.1.refs_4_
  21.9 0.9 slice_reduce_fusion.2
  22.7 0.6 collective-permute-done.2.refs_5_
  23.4 0.9 slice_reduce_fusion.1
  24.3 0.1 concatenate.3
  24.4 20.8 %first_step.1 = (f32[10,8,128,128]{3,2,1,0:T(8,128)}, f32[120,384]{1,0:T(8,128)S(1)}, f32[120,384]{1,0:T(8,128)S(1)}, f32[1320,128]{1,0:T(8,128)S(1)}, f32[1392,128]{1,0:T(8,128)S(1)}, /*index=5*/s32[42]{0:T(128)S(1)}) custom-call(s32[120]{0:T(128)S(1)} %compare_select_fusion.2.refs_0_, bf16[384,2048]{1,0:T(8,128)(2,1)S(1)} %get-tuple-element.23.refs_1_, ...), custom_call_target="tpu_custom_call" | custom-call | flops 400000000 | bytes 16777216 | tf_op jit(solution)/shard_map/first_step/pallas_call | solution.py:521
  45.2 4.2 %collective-permute-start.5 = (f32[1392,128]{1,0:T(8,128)S(1)}, f32[1392,128]{1,0:T(8,128)S(1)}, u32[]{:S(2)}, u32[]{:S(2)}) collective-permute-start(f32[1392,128]{1,0:T(8,128)S(1)} %get-tuple-element.27), channel_id=1, source_target_pairs={{1,0},{2,1},{3,2},{4,3},{5,4},{6,5},{7,6},{8,7},{9,8},{10,9},{11,1... | collective-permute-start | bytes 2138120 | tf_op jit(solution)/shard_map/ppermute | solution.py:51
  49.4 0.0 collective-permute-start.4
  49.4 8.9 %collective-permute-done.4.refs_4_ = f32[1320,128]{1,0:T(8,128)S(1)} collective-permute-done((f32[1320,128]{1,0:T(8,128)S(1)}, f32[1320,128]{1,0:T(8,128)S(1)}, u32[]{:S(2)}, u32[]{:S(2)}) %collective-permute-start.4) | collective-permute-done | bytes 675872 | tf_op jit(solution)/shard_map/ppermute | solution.py:51
  58.4 18.7 %step.1 = (f32[10,8,128,128]{3,2,1,0:T(8,128)}, f32[120,384]{1,0:T(8,128)S(1)}, f32[120,384]{1,0:T(8,128)S(1)}, f32[1320,128]{1,0:T(8,128)S(1)}, f32[1392,128]{1,0:T(8,128)S(1)}) custom-call(s32[120]{0:T(128)S(1)} %compare_select_fusion.2.refs_0_, bf16[384,2048]{1,0:T(8,128)(2,1)S(1)} %get-tuple-element.23.refs_1_, ...), custom_call_target="tpu_custom_call", output_to_operand_aliasing={{0}: (3, {})} | custom-call | flops 400000000 | bytes 16777216 | tf_op jit(solution)/shard_map/step/pallas_call | solution.py:521
  77.0 13.0 %collective-permute-start.7 = (f32[1392,128]{1,0:T(8,128)S(1)}, f32[1392,128]{1,0:T(8,128)S(1)}, u32[]{:S(2)}, u32[]{:S(2)}) collective-permute-start(f32[1392,128]{1,0:T(8,128)S(1)} %get-tuple-element.33), channel_id=1, source_target_pairs={{1,0},{2,1},{3,2},{4,3},{5,4},{6,5},{7,6},{8,7},{9,8},{10,9},{11,1... | collective-permute-start | bytes 2138120 | tf_op jit(solution)/shard_map/ppermute | solution.py:51
  90.0 7.7 %collective-permute-done.6.refs_4_ = f32[1320,128]{1,0:T(8,128)S(1)} collective-permute-done((f32[1320,128]{1,0:T(8,128)S(1)}, f32[1320,128]{1,0:T(8,128)S(1)}, u32[]{:S(2)}, u32[]{:S(2)}) %collective-permute-start.6) | collective-permute-done | bytes 675872 | tf_op jit(solution)/shard_map/ppermute | solution.py:51
  97.8 18.7 %last_step.1 = (f32[10,8,128,128]{3,2,1,0:T(8,128)}, f32[120,384]{1,0:T(8,128)S(1)}) custom-call(s32[120]{0:T(128)S(1)} %compare_select_fusion.2.refs_0_, bf16[384,2048]{1,0:T(8,128)(2,1)S(1)} %get-tuple-element.23.refs_1_, bf16[384,2048]{1,0:T(8,128)(2,1)S(1)} %get-tuple-element.24.refs_2_, ...), custom_call_target="tpu_custom_call", output_to_operand_aliasing={{0}: (3, {})} | custom-call | flops 400000000 | bytes 16777216 | tf_op jit(solution)/shard_map/last_step/pallas_call | solution.py:521
  116.5 2.5 %collective-permute-start.8 = (f32[24,384]{1,0:T(8,128)S(1)}, f32[24,384]{1,0:T(8,128)S(1)}, u32[]{:S(2)}, u32[]{:S(2)}) collective-permute-start(f32[24,384]{1,0:T(8,128)S(1)} %get-tuple-element.38), channel_id=1, source_target_pairs={{127,0},{0,1},{1,2},{2,3},{3,4},{4,5},{5,6},{6,7},{7,8},{8,9},{9,1... | collective-permute-start | bytes 110600 | tf_op jit(solution)/shard_map/ppermute | solution.py:51
  119.0 11.5 %collective-permute-start.10 = (f32[24,384]{1,0:T(8,128)S(1)}, f32[24,384]{1,0:T(8,128)S(1)}, u32[]{:S(2)}, u32[]{:S(2)}) collective-permute-start(f32[24,384]{1,0:T(8,128)S(1)} %get-tuple-element.39), channel_id=1, source_target_pairs={{2,0},{3,1},{4,2},{5,3},{6,4},{7,5},{8,6},{9,7},{10,8},{11,9},{12,... | collective-permute-start | bytes 110600 | tf_op jit(solution)/shard_map/ppermute | solution.py:51
  130.6 1.1 collective-permute-done.10
  131.6 2.3 %collective-permute-done.9 = f32[24,384]{1,0:T(8,128)S(1)} collective-permute-done((f32[24,384]{1,0:T(8,128)S(1)}, f32[24,384]{1,0:T(8,128)S(1)}, u32[]{:S(2)}, u32[]{:S(2)}) %collective-permute-start.9) | collective-permute-done | bytes 36896 | tf_op jit(solution)/shard_map/ppermute | solution.py:51
  134.0 0.6 fusion.1
  (15 shorter events, 0.1 us)
Async XLA Ops:
  0.6 13.6 %copy-start.2 = (f32[512,289]{0,1:T(8,128)S(1)}, f32[512,289]{0,1:T(8,128)}, u32[]{:S(2)}) copy-start(f32[512,289]{0,1:T(8,128)} %param.8) | copy-start | bytes 1775620
  3.8 18.0 %collective-permute-start.1 = (f32[1224,128]{1,0:T(8,128)}, f32[1224,128]{1,0:T(8,128)}, u32[]{:S(2)}, u32[]{:S(2)}) collective-permute-start(f32[1224,128]{1,0:T(8,128)} %get-tuple-element.21), channel_id=1, source_target_pairs={{127,0},{0,1},{1,2},{2,3},{3,4},{4,5},{5,6},{6,7},{7,8},{8,9},{9,1... | collective-permute-start | bytes 1880072 | tf_op jit(solution)/shard_map/ppermute | solution.py:51
  6.9 12.2 %collective-permute-start.3 = (f32[24,384]{1,0:T(8,128)}, f32[24,384]{1,0:T(8,128)S(1)}, u32[]{:S(2)}, u32[]{:S(2)}) collective-permute-start(f32[24,384]{1,0:T(8,128)} %get-tuple-element.20.refs_6_), channel_id=1, source_target_pairs={{2,0},{3,1},{4,2},{5,3},{6,4},{7,5},{8,6},{9,7},{10,8},{11,9},{12,... | collective-permute-start | bytes 110600 | tf_op jit(solution)/shard_map/ppermute | solution.py:51
  13.2 8.4 %collective-permute-start = (f32[24,384]{1,0:T(8,128)}, f32[24,384]{1,0:T(8,128)S(1)}, u32[]{:S(2)}, u32[]{:S(2)}) collective-permute-start(f32[24,384]{1,0:T(8,128)} %get-tuple-element.20.refs_6_), channel_id=1, source_target_pairs={{126,0},{127,1},{0,2},{1,3},{2,4},{3,5},{4,6},{5,7},{6,8},{7,9},{8... | collective-permute-start | bytes 110600 | tf_op jit(solution)/shard_map/ppermute | solution.py:51
  13.2 10.2 %collective-permute-start.2 = (f32[1224,128]{1,0:T(8,128)}, f32[1224,128]{1,0:T(8,128)}, u32[]{:S(2)}, u32[]{:S(2)}) collective-permute-start(f32[1224,128]{1,0:T(8,128)} %get-tuple-element.22), channel_id=1, source_target_pairs={{1,0},{2,1},{3,2},{4,3},{5,4},{6,5},{7,6},{8,7},{9,8},{10,9},{11,1... | collective-permute-start | bytes 1880072 | tf_op jit(solution)/shard_map/ppermute | solution.py:51
  14.5 4.5 %copy-start = (f32[24,384]{1,0:T(8,128)S(1)}, f32[24,384]{1,0:T(8,128)}, u32[]{:S(2)}) copy-start(f32[24,384]{1,0:T(8,128)} %get-tuple-element.20.refs_6_) | copy-start | bytes 110596
  14.5 2.2 %copy-start.1 = (f32[512,2048]{1,0:T(8,128)S(1)}, f32[512,2048]{1,0:T(8,128)}, u32[]{:S(2)}) copy-start(f32[512,2048]{1,0:T(8,128)} %spreading_ref.1) | copy-start | bytes 12582916
  45.2 13.2 %collective-permute-start.5 = (f32[1392,128]{1,0:T(8,128)S(1)}, f32[1392,128]{1,0:T(8,128)S(1)}, u32[]{:S(2)}, u32[]{:S(2)}) collective-permute-start(f32[1392,128]{1,0:T(8,128)S(1)} %get-tuple-element.27), channel_id=1, source_target_pairs={{1,0},{2,1},{3,2},{4,3},{5,4},{6,5},{7,6},{8,7},{9,8},{10,9},{11,1... | collective-permute-start | bytes 2138120 | tf_op jit(solution)/shard_map/ppermute | solution.py:51
  49.4 9.0 %collective-permute-start.4 = (f32[1320,128]{1,0:T(8,128)S(1)}, f32[1320,128]{1,0:T(8,128)S(1)}, u32[]{:S(2)}, u32[]{:S(2)}) collective-permute-start(f32[1320,128]{1,0:T(8,128)S(1)} %get-tuple-element.26), channel_id=1, source_target_pairs={{127,0},{0,1},{1,2},{2,3},{3,4},{4,5},{5,6},{6,7},{7,8},{8,9},{9,1... | collective-permute-start | bytes 2027528 | tf_op jit(solution)/shard_map/ppermute | solution.py:51
  77.0 20.8 %collective-permute-start.7 = (f32[1392,128]{1,0:T(8,128)S(1)}, f32[1392,128]{1,0:T(8,128)S(1)}, u32[]{:S(2)}, u32[]{:S(2)}) collective-permute-start(f32[1392,128]{1,0:T(8,128)S(1)} %get-tuple-element.33), channel_id=1, source_target_pairs={{1,0},{2,1},{3,2},{4,3},{5,4},{6,5},{7,6},{8,7},{9,8},{10,9},{11,1... | collective-permute-start | bytes 2138120 | tf_op jit(solution)/shard_map/ppermute | solution.py:51
  90.0 7.8 %collective-permute-start.6 = (f32[1320,128]{1,0:T(8,128)S(1)}, f32[1320,128]{1,0:T(8,128)S(1)}, u32[]{:S(2)}, u32[]{:S(2)}) collective-permute-start(f32[1320,128]{1,0:T(8,128)S(1)} %get-tuple-element.32), channel_id=1, source_target_pairs={{127,0},{0,1},{1,2},{2,3},{3,4},{4,5},{5,6},{6,7},{7,8},{8,9},{9,1... | collective-permute-start | bytes 2027528 | tf_op jit(solution)/shard_map/ppermute | solution.py:51
  97.8 36.2 %copy-start.3 = (f32[8,3,289]{2,0,1:T(8,128)S(1)}, f32[8,3,289]{2,0,1:T(8,128)}, u32[]{:S(2)}) copy-start(f32[8,3,289]{2,0,1:T(8,128)} %param.6) | copy-start | bytes 83236
  116.5 14.1 %collective-permute-start.8 = (f32[24,384]{1,0:T(8,128)S(1)}, f32[24,384]{1,0:T(8,128)S(1)}, u32[]{:S(2)}, u32[]{:S(2)}) collective-permute-start(f32[24,384]{1,0:T(8,128)S(1)} %get-tuple-element.38), channel_id=1, source_target_pairs={{127,0},{0,1},{1,2},{2,3},{3,4},{4,5},{5,6},{6,7},{7,8},{8,9},{9,1... | collective-permute-start | bytes 110600 | tf_op jit(solution)/shard_map/ppermute | solution.py:51
  119.0 12.6 %collective-permute-start.10 = (f32[24,384]{1,0:T(8,128)S(1)}, f32[24,384]{1,0:T(8,128)S(1)}, u32[]{:S(2)}, u32[]{:S(2)}) collective-permute-start(f32[24,384]{1,0:T(8,128)S(1)} %get-tuple-element.39), channel_id=1, source_target_pairs={{2,0},{3,1},{4,2},{5,3},{6,4},{7,5},{8,6},{9,7},{10,8},{11,9},{12,... | collective-permute-start | bytes 110600 | tf_op jit(solution)/shard_map/ppermute | solution.py:51
  130.5 3.4 %collective-permute-start.9 = (f32[24,384]{1,0:T(8,128)S(1)}, f32[24,384]{1,0:T(8,128)S(1)}, u32[]{:S(2)}, u32[]{:S(2)}) collective-permute-start(f32[24,384]{1,0:T(8,128)S(1)} %get-tuple-element.40), channel_id=1, source_target_pairs={{1,0},{2,1},{3,2},{4,3},{5,4},{6,5},{7,6},{8,7},{9,8},{10,9},{11,1... | collective-permute-start | bytes 110600 | tf_op jit(solution)/shard_map/ppermute | solution.py:51

commit v2 on v1

--- a/solution.py
+++ b/solution.py
@@ -20,6 +20,7 @@
 OWNED = 8
 COEFS = 289
 SLOTS = 40
+ORDER = 48
 LANES = 384
 KEPT = 304
 CELLS = 2048
@@ -37,6 +38,8 @@
 DEPTH = PLANES + 2 * BZ + 1
 BOXED = ROWS + 1
 CHUNK = 16
+WIDE = 64
+BATCH = 4
 JK = ((0, 0), (1, 0), (2, 0), (0, 1), (1, 1), (0, 2))
 
 VMEM = pl.BlockSpec(memory_space=pltpu.VMEM)
@@ -243,9 +246,10 @@
             return count + near.astype(jnp.int32), jnp.where(near, spare, slot)
 
         count, spare = lax.fori_loop(0, SLOTS, scan, (jnp.int32(0), jnp.int32(0)))
-        order_ref[count] = spare
-        order_ref[SLOTS + 1] = (count + 1) // 2
-    pairs = order_ref[SLOTS + 1]
+        for n in range(BATCH - 1):
+            order_ref[count + n] = spare
+        order_ref[ORDER - 1] = (count + BATCH - 1) // BATCH
+    rounds = order_ref[ORDER - 1]
 
     for c in range(3):
         start = (c * DEPTH + BZ - 1) * PITCH
@@ -313,10 +317,10 @@
         rows = [half * 8 * BOXED + base + c * OWNED for c in range(3) for half in range(2)]
         return above, spots, starts, rows
 
-    def place_pair(pair, carry):
+    def place_batch(batch, carry):
         found = []
-        for n in range(2):
-            _, spots, starts, rows = box_parts(order_ref[pair * 2 + n])
+        for n in range(BATCH):
+            _, spots, starts, rows = box_parts(order_ref[batch * BATCH + n])
             cells = jnp.concatenate([boxes[pl.ds(start, 8, stride=BOXED)] for start in rows], axis=0)
             placed = jnp.dot(
                 jnp.concatenate(split(cells), axis=1),
@@ -335,7 +339,7 @@
                 force[there] = value
         return carry
 
-    lax.fori_loop(0, pairs, place_pair, 0)
+    lax.fori_loop(0, rounds, place_batch, 0)
 
     def fold(z, carry):
         for c in range(3):
@@ -353,11 +357,11 @@
 
 
         def collide_chunk(step, carry):
-            y = pl.multiple_of(step * CHUNK, CHUNK)
-            rows = pl.ds(y, CHUNK)
+            y = pl.multiple_of(step * WIDE, WIDE)
+            rows = pl.ds(y, WIDE)
             m = [old[f, z, rows] for f in range(FIELDS)]
             cell, line, square, cross = collide_rows(
-                m, [force[pl.ds((c * DEPTH + z + BZ - 1) * PITCH + y, CHUNK)] for c in range(3)]
+                m, [force[pl.ds((c * DEPTH + z + BZ - 1) * PITCH + y, WIDE)] for c in range(3)]
             )
             even = [
                 spread_x(cell, line[2], square[2]),
@@ -366,7 +370,7 @@
             ]
             twice = spread_x(square[0], None, None)
             odd = [spread_x(line[0], cross[1], None), spread_x(cross[0], None, None)]
-            moved = pl.ds(y + 8, CHUNK)
+            moved = pl.ds(y + 8, WIDE)
             for k in range(3):
                 ends = even[0][k] + even[2][k]
                 shifts[k, moved] = ends + even[1][k]
@@ -378,7 +382,7 @@
                 stills[3 + k, rows] = 4.0 * odd[0][k]
             return carry
 
-        lax.fori_loop(0, SIDE // CHUNK, collide_chunk, 0)
+        lax.fori_loop(0, SIDE // WIDE, collide_chunk, 0)
         for field in range(15):
             shifts[field, 7:8] = shifts[field, SIDE + 7 : SIDE + 8]
             shifts[field, SIDE + 8 : SIDE + 9] = shifts[field, 8:9]
@@ -443,10 +447,10 @@
         lax.dot_general, dimension_numbers=(((1,), (1,)), ((), ())), preferred_element_type=F32
     )
 
-    def sample_pair(pair, carry):
+    def sample_batch(batch, carry):
         results = []
-        for n in range(2):
-            above, spots, starts, rows = box_parts(order_ref[pair * 2 + n])
+        for n in range(BATCH):
+            above, spots, starts, rows = box_parts(order_ref[batch * BATCH + n])
             cells = jnp.concatenate(
                 [
                     jnp.concatenate([velocity[pl.ds(start + i, 8, stride=PITCH)] for i in range(8)], axis=1)
@@ -463,7 +467,7 @@
                 sampled[pl.ds(start, 8, stride=BOXED)] = jnp.where(ours, value, 0.0)
         return carry
 
-    lax.fori_loop(0, pairs, sample_pair, 0)
+    lax.fori_loop(0, rounds, sample_batch, 0)
 
     part_high, part_low = split(
         jnp.concatenate([sampled[chunk_row(n) : chunk_row(n) + ROWS] for n in range(16)], axis=1)
@@ -501,7 +505,7 @@
         ]
         out_specs += [VMEM] * 3
     if first:
-        out_shape.append(jax.ShapeDtypeStruct((SLOTS + 2,), jnp.int32))
+        out_shape.append(jax.ShapeDtypeStruct((ORDER,), jnp.int32))
         out_specs.append(SMEM)
     scratch = [
         pltpu.VMEM((FIELDS, PLANES + 2) + square, F32),

time: 135 us -> 120 us (0.89)
  Pallas kernels: 63.5 us -> 47.3 us
    pallas_call x3, Pallas kernels: 58.2 us -> 41.9 us  [advance(): pl.pallas_call(functools.partial(step_kernel, first, last), out_shape=out...]
where the time goes in v2:
time: 120 us; the launch traced here: 119 us
  Pallas kernels  47.3 us (39%)
  starting transfers between devices  42.5 us (35%)
  waiting for transfers between devices  23.1 us (19%)
  local copies, waits for them, and re-layouts  4.92 us (4%)
    ppermute x11, starting transfers between devices, shifted(): lax.ppermute(block, 'gz', [((i - distance) % devices, i) for i in range(d...  42.5 us
    pallas_call x3, Pallas kernels, advance(): pl.pallas_call(functools.partial(step_kernel, first, last), out_shape=out...  41.9 us
    ppermute x11, waiting for transfers between devices, shifted(): lax.ppermute(block, 'gz', [((i - distance) % devices, i) for i in range(d...  23.1 us
    pallas_call x1, Pallas kernels, pack(): pl.pallas_call(pack_kernel, out_shape=(jax.ShapeDtypeStruct((GROUP, LANES...  3.2 us
    unnamed x9, local copies, waits for them, and re-layouts  2.46 us
  transfers between devices with their start and end apart: 11, of which 6 were waited for; matrix products, arithmetic and copies ran while one was open for 1% of the time, Pallas kernels for 2%

profile of v2, /device:TPU:1, one launch (start us, length us, event | category | flops | bytes accessed | tf_op | source)
XLA Modules:
  0.0 119.3 jit_solution(14643844349972118228)
XLA Ops:
  0.6 3.2 %pack.1 = (f32[24,384]{1,0:T(8,128)}, f32[1224,128]{1,0:T(8,128)}, f32[1224,128]{1,0:T(8,128)}) custom-call(s32[3,8]{1,0:T(4,128)} %bitcast.9, f32[10,8,128,128]{3,2,1,0:T(8,128)} %refs_3_.1, f32[3,8,289]{2,1,0:T(8,128)} %bitcast.8), custom_call_target="tpu_custom_call" | custom-call | tf_op jit(solution)/shard_map/pack/pallas_call | solution.py:169
  3.8 3.1 %collective-permute-start.1 = (f32[1224,128]{1,0:T(8,128)}, f32[1224,128]{1,0:T(8,128)}, u32[]{:S(2)}, u32[]{:S(2)}) collective-permute-start(f32[1224,128]{1,0:T(8,128)} %get-tuple-element.21), channel_id=1, source_target_pairs={{127,0},{0,1},{1,2},{2,3},{3,4},{4,5},{5,6},{6,7},{7,8},{8,9},{9,1... | collective-permute-start | bytes 1880072 | tf_op jit(solution)/shard_map/ppermute | solution.py:54
  6.9 6.3 %collective-permute-start.3 = (f32[24,384]{1,0:T(8,128)}, f32[24,384]{1,0:T(8,128)S(1)}, u32[]{:S(2)}, u32[]{:S(2)}) collective-permute-start(f32[24,384]{1,0:T(8,128)} %get-tuple-element.20.refs_6_), channel_id=1, source_target_pairs={{2,0},{3,1},{4,2},{5,3},{6,4},{7,5},{8,6},{9,7},{10,8},{11,9},{12,... | collective-permute-start | bytes 110600 | tf_op jit(solution)/shard_map/ppermute | solution.py:54
  13.2 1.0 collective-permute-start.2
  14.2 0.3 copy.10
  14.5 0.0 copy-start
  14.5 0.1 pad.4.synthesis_ref
  14.5 0.0 copy-start.1
  14.5 2.2 %copy-done.1 = f32[512,2048]{1,0:T(8,128)S(1)} copy-done((f32[512,2048]{1,0:T(8,128)S(1)}, f32[512,2048]{1,0:T(8,128)}, u32[]{:S(2)}) %copy-start.1) | copy-done | bytes 4194328
  16.7 2.2 %couple.1 = (bf16[384,2048]{1,0:T(8,128)(2,1)S(1)}, bf16[384,2048]{1,0:T(8,128)(2,1)S(1)}) custom-call(f32[512,384]{1,0:T(8,128)S(1)} %pad.4.synthesis_ref, f32[512,2048]{1,0:T(8,128)S(1)} %copy-done.1), custom_call_target="tpu_custom_call" | custom-call | flops 2415919104 | bytes 8388608 | tf_op jit(solution)/shard_map/couple/pallas_call | solution.py:129
  18.9 0.2 slice_reduce_fusion.4
  19.1 0.2 slice_reduce_fusion
  19.3 2.4 %collective-permute-done.refs_7_ = f32[24,384]{1,0:T(8,128)S(1)} collective-permute-done((f32[24,384]{1,0:T(8,128)}, f32[24,384]{1,0:T(8,128)S(1)}, u32[]{:S(2)}, u32[]{:S(2)}) %collective-permute-start) | collective-permute-done | bytes 36896 | tf_op jit(solution)/shard_map/ppermute | solution.py:54
  21.7 0.2 slice_reduce_fusion.3
  21.9 0.0 collective-permute-done.1.refs_4_
  21.9 0.9 slice_reduce_fusion.2
  22.7 0.6 collective-permute-done.2.refs_5_
  23.4 0.9 slice_reduce_fusion.1
  24.3 0.1 concatenate.3
  24.4 15.5 %first_step.1 = (f32[10,8,128,128]{3,2,1,0:T(8,128)}, f32[120,384]{1,0:T(8,128)S(1)}, f32[120,384]{1,0:T(8,128)S(1)}, f32[1320,128]{1,0:T(8,128)S(1)}, f32[1392,128]{1,0:T(8,128)S(1)}, /*index=5*/s32[48]{0:T(128)S(1)}) custom-call(s32[120]{0:T(128)S(1)} %compare_select_fusion.2.refs_0_, bf16[384,2048]{1,0:T(8,128)(2,1)S(1)} %get-tuple-element.23.refs_1_, ...), custom_call_target="tpu_custom_call" | custom-call | flops 400000000 | bytes 16777216 | tf_op jit(solution)/shard_map/first_step/pallas_call | solution.py:525
  39.8 4.5 %collective-permute-start.5 = (f32[1392,128]{1,0:T(8,128)S(1)}, f32[1392,128]{1,0:T(8,128)S(1)}, u32[]{:S(2)}, u32[]{:S(2)}) collective-permute-start(f32[1392,128]{1,0:T(8,128)S(1)} %get-tuple-element.27), channel_id=1, source_target_pairs={{1,0},{2,1},{3,2},{4,3},{5,4},{6,5},{7,6},{8,7},{9,8},{10,9},{11,1... | collective-permute-start | bytes 2138120 | tf_op jit(solution)/shard_map/ppermute | solution.py:54
  44.3 9.0 %collective-permute-done.4.refs_4_ = f32[1320,128]{1,0:T(8,128)S(1)} collective-permute-done((f32[1320,128]{1,0:T(8,128)S(1)}, f32[1320,128]{1,0:T(8,128)S(1)}, u32[]{:S(2)}, u32[]{:S(2)}) %collective-permute-start.4) | collective-permute-done | bytes 675872 | tf_op jit(solution)/shard_map/ppermute | solution.py:54
  53.3 13.3 %step.1 = (f32[10,8,128,128]{3,2,1,0:T(8,128)}, f32[120,384]{1,0:T(8,128)S(1)}, f32[120,384]{1,0:T(8,128)S(1)}, f32[1320,128]{1,0:T(8,128)S(1)}, f32[1392,128]{1,0:T(8,128)S(1)}) custom-call(s32[120]{0:T(128)S(1)} %compare_select_fusion.2.refs_0_, bf16[384,2048]{1,0:T(8,128)(2,1)S(1)} %get-tuple-element.23.refs_1_, ...), custom_call_target="tpu_custom_call", output_to_operand_aliasing={{0}: (3, {})} | custom-call | flops 400000000 | bytes 16777216 | tf_op jit(solution)/shard_map/step/pallas_call | solution.py:525
  66.6 13.3 %collective-permute-start.7 = (f32[1392,128]{1,0:T(8,128)S(1)}, f32[1392,128]{1,0:T(8,128)S(1)}, u32[]{:S(2)}, u32[]{:S(2)}) collective-permute-start(f32[1392,128]{1,0:T(8,128)S(1)} %get-tuple-element.33), channel_id=1, source_target_pairs={{1,0},{2,1},{3,2},{4,3},{5,4},{6,5},{7,6},{8,7},{9,8},{10,9},{11,1... | collective-permute-start | bytes 2138120 | tf_op jit(solution)/shard_map/ppermute | solution.py:54
  79.9 0.0 collective-permute-start.6
  79.9 7.7 %collective-permute-done.6.refs_4_ = f32[1320,128]{1,0:T(8,128)S(1)} collective-permute-done((f32[1320,128]{1,0:T(8,128)S(1)}, f32[1320,128]{1,0:T(8,128)S(1)}, u32[]{:S(2)}, u32[]{:S(2)}) %collective-permute-start.6) | collective-permute-done | bytes 675872 | tf_op jit(solution)/shard_map/ppermute | solution.py:54
  87.7 13.2 %last_step.1 = (f32[10,8,128,128]{3,2,1,0:T(8,128)}, f32[120,384]{1,0:T(8,128)S(1)}) custom-call(s32[120]{0:T(128)S(1)} %compare_select_fusion.2.refs_0_, bf16[384,2048]{1,0:T(8,128)(2,1)S(1)} %get-tuple-element.23.refs_1_, bf16[384,2048]{1,0:T(8,128)(2,1)S(1)} %get-tuple-element.24.refs_2_, ...), custom_call_target="tpu_custom_call", output_to_operand_aliasing={{0}: (3, {})} | custom-call | flops 400000000 | bytes 16777216 | tf_op jit(solution)/shard_map/last_step/pallas_call | solution.py:525
  100.9 2.6 %collective-permute-start.8 = (f32[24,384]{1,0:T(8,128)S(1)}, f32[24,384]{1,0:T(8,128)S(1)}, u32[]{:S(2)}, u32[]{:S(2)}) collective-permute-start(f32[24,384]{1,0:T(8,128)S(1)} %get-tuple-element.38), channel_id=1, source_target_pairs={{127,0},{0,1},{1,2},{2,3},{3,4},{4,5},{5,6},{6,7},{7,8},{8,9},{9,1... | collective-permute-start | bytes 110600 | tf_op jit(solution)/shard_map/ppermute | solution.py:54
  103.4 11.8 %collective-permute-start.10 = (f32[24,384]{1,0:T(8,128)S(1)}, f32[24,384]{1,0:T(8,128)S(1)}, u32[]{:S(2)}, u32[]{:S(2)}) collective-permute-start(f32[24,384]{1,0:T(8,128)S(1)} %get-tuple-element.39), channel_id=1, source_target_pairs={{2,0},{3,1},{4,2},{5,3},{6,4},{7,5},{8,6},{9,7},{10,8},{11,9},{12,... | collective-permute-start | bytes 110600 | tf_op jit(solution)/shard_map/ppermute | solution.py:54
  115.2 1.1 collective-permute-done.10
  116.3 2.3 %collective-permute-done.9 = f32[24,384]{1,0:T(8,128)S(1)} collective-permute-done((f32[24,384]{1,0:T(8,128)S(1)}, f32[24,384]{1,0:T(8,128)S(1)}, u32[]{:S(2)}, u32[]{:S(2)}) %collective-permute-start.9) | collective-permute-done | bytes 36896 | tf_op jit(solution)/shard_map/ppermute | solution.py:54
  118.6 0.6 fusion.1
  (15 shorter events, 0.1 us)
Async XLA Ops:
  0.6 13.6 %copy-start.2 = (f32[512,289]{0,1:T(8,128)S(1)}, f32[512,289]{0,1:T(8,128)}, u32[]{:S(2)}) copy-start(f32[512,289]{0,1:T(8,128)} %param.8) | copy-start | bytes 1775620
  3.8 18.0 %collective-permute-start.1 = (f32[1224,128]{1,0:T(8,128)}, f32[1224,128]{1,0:T(8,128)}, u32[]{:S(2)}, u32[]{:S(2)}) collective-permute-start(f32[1224,128]{1,0:T(8,128)} %get-tuple-element.21), channel_id=1, source_target_pairs={{127,0},{0,1},{1,2},{2,3},{3,4},{4,5},{5,6},{6,7},{7,8},{8,9},{9,1... | collective-permute-start | bytes 1880072 | tf_op jit(solution)/shard_map/ppermute | solution.py:54
  6.9 12.2 %collective-permute-start.3 = (f32[24,384]{1,0:T(8,128)}, f32[24,384]{1,0:T(8,128)S(1)}, u32[]{:S(2)}, u32[]{:S(2)}) collective-permute-start(f32[24,384]{1,0:T(8,128)} %get-tuple-element.20.refs_6_), channel_id=1, source_target_pairs={{2,0},{3,1},{4,2},{5,3},{6,4},{7,5},{8,6},{9,7},{10,8},{11,9},{12,... | collective-permute-start | bytes 110600 | tf_op jit(solution)/shard_map/ppermute | solution.py:54
  13.2 8.4 %collective-permute-start = (f32[24,384]{1,0:T(8,128)}, f32[24,384]{1,0:T(8,128)S(1)}, u32[]{:S(2)}, u32[]{:S(2)}) collective-permute-start(f32[24,384]{1,0:T(8,128)} %get-tuple-element.20.refs_6_), channel_id=1, source_target_pairs={{126,0},{127,1},{0,2},{1,3},{2,4},{3,5},{4,6},{5,7},{6,8},{7,9},{8... | collective-permute-start | bytes 110600 | tf_op jit(solution)/shard_map/ppermute | solution.py:54
  13.2 10.2 %collective-permute-start.2 = (f32[1224,128]{1,0:T(8,128)}, f32[1224,128]{1,0:T(8,128)}, u32[]{:S(2)}, u32[]{:S(2)}) collective-permute-start(f32[1224,128]{1,0:T(8,128)} %get-tuple-element.22), channel_id=1, source_target_pairs={{1,0},{2,1},{3,2},{4,3},{5,4},{6,5},{7,6},{8,7},{9,8},{10,9},{11,1... | collective-permute-start | bytes 1880072 | tf_op jit(solution)/shard_map/ppermute | solution.py:54
  14.5 4.5 %copy-start = (f32[24,384]{1,0:T(8,128)S(1)}, f32[24,384]{1,0:T(8,128)}, u32[]{:S(2)}) copy-start(f32[24,384]{1,0:T(8,128)} %get-tuple-element.20.refs_6_) | copy-start | bytes 110596
  14.5 2.2 %copy-start.1 = (f32[512,2048]{1,0:T(8,128)S(1)}, f32[512,2048]{1,0:T(8,128)}, u32[]{:S(2)}) copy-start(f32[512,2048]{1,0:T(8,128)} %spreading_ref.1) | copy-start | bytes 12582916
  39.8 13.5 %collective-permute-start.5 = (f32[1392,128]{1,0:T(8,128)S(1)}, f32[1392,128]{1,0:T(8,128)S(1)}, u32[]{:S(2)}, u32[]{:S(2)}) collective-permute-start(f32[1392,128]{1,0:T(8,128)S(1)} %get-tuple-element.27), channel_id=1, source_target_pairs={{1,0},{2,1},{3,2},{4,3},{5,4},{6,5},{7,6},{8,7},{9,8},{10,9},{11,1... | collective-permute-start | bytes 2138120 | tf_op jit(solution)/shard_map/ppermute | solution.py:54
  44.3 9.0 %collective-permute-start.4 = (f32[1320,128]{1,0:T(8,128)S(1)}, f32[1320,128]{1,0:T(8,128)S(1)}, u32[]{:S(2)}, u32[]{:S(2)}) collective-permute-start(f32[1320,128]{1,0:T(8,128)S(1)} %get-tuple-element.26), channel_id=1, source_target_pairs={{127,0},{0,1},{1,2},{2,3},{3,4},{4,5},{5,6},{6,7},{7,8},{8,9},{9,1... | collective-permute-start | bytes 2027528 | tf_op jit(solution)/shard_map/ppermute | solution.py:54
  66.6 21.1 %collective-permute-start.7 = (f32[1392,128]{1,0:T(8,128)S(1)}, f32[1392,128]{1,0:T(8,128)S(1)}, u32[]{:S(2)}, u32[]{:S(2)}) collective-permute-start(f32[1392,128]{1,0:T(8,128)S(1)} %get-tuple-element.33), channel_id=1, source_target_pairs={{1,0},{2,1},{3,2},{4,3},{5,4},{6,5},{7,6},{8,7},{9,8},{10,9},{11,1... | collective-permute-start | bytes 2138120 | tf_op jit(solution)/shard_map/ppermute | solution.py:54
  79.9 7.8 %collective-permute-start.6 = (f32[1320,128]{1,0:T(8,128)S(1)}, f32[1320,128]{1,0:T(8,128)S(1)}, u32[]{:S(2)}, u32[]{:S(2)}) collective-permute-start(f32[1320,128]{1,0:T(8,128)S(1)} %get-tuple-element.32), channel_id=1, source_target_pairs={{127,0},{0,1},{1,2},{2,3},{3,4},{4,5},{5,6},{6,7},{7,8},{8,9},{9,1... | collective-permute-start | bytes 2027528 | tf_op jit(solution)/shard_map/ppermute | solution.py:54
  87.7 30.9 %copy-start.3 = (f32[8,3,289]{2,0,1:T(8,128)S(1)}, f32[8,3,289]{2,0,1:T(8,128)}, u32[]{:S(2)}) copy-start(f32[8,3,289]{2,0,1:T(8,128)} %param.6) | copy-start | bytes 83236
  100.9 14.4 %collective-permute-start.8 = (f32[24,384]{1,0:T(8,128)S(1)}, f32[24,384]{1,0:T(8,128)S(1)}, u32[]{:S(2)}, u32[]{:S(2)}) collective-permute-start(f32[24,384]{1,0:T(8,128)S(1)} %get-tuple-element.38), channel_id=1, source_target_pairs={{127,0},{0,1},{1,2},{2,3},{3,4},{4,5},{5,6},{6,7},{7,8},{8,9},{9,1... | collective-permute-start | bytes 110600 | tf_op jit(solution)/shard_map/ppermute | solution.py:54
  103.4 12.9 %collective-permute-start.10 = (f32[24,384]{1,0:T(8,128)S(1)}, f32[24,384]{1,0:T(8,128)S(1)}, u32[]{:S(2)}, u32[]{:S(2)}) collective-permute-start(f32[24,384]{1,0:T(8,128)S(1)} %get-tuple-element.39), channel_id=1, source_target_pairs={{2,0},{3,1},{4,2},{5,3},{6,4},{7,5},{8,6},{9,7},{10,8},{11,9},{12,... | collective-permute-start | bytes 110600 | tf_op jit(solution)/shard_map/ppermute | solution.py:54
  115.2 3.4 %collective-permute-start.9 = (f32[24,384]{1,0:T(8,128)S(1)}, f32[24,384]{1,0:T(8,128)S(1)}, u32[]{:S(2)}, u32[]{:S(2)}) collective-permute-start(f32[24,384]{1,0:T(8,128)S(1)} %get-tuple-element.40), channel_id=1, source_target_pairs={{1,0},{2,1},{3,2},{4,3},{5,4},{6,5},{7,6},{8,7},{9,8},{10,9},{11,1... | collective-permute-start | bytes 110600 | tf_op jit(solution)/shard_map/ppermute | solution.py:54

commit v3 on v2

--- a/solution.py
+++ b/solution.py
@@ -38,7 +38,8 @@
 DEPTH = PLANES + 2 * BZ + 1
 BOXED = ROWS + 1
 CHUNK = 16
-WIDE = 64
+WIDE = 16
+UNROLL = 8
 BATCH = 4
 JK = ((0, 0), (1, 0), (2, 0), (0, 1), (1, 1), (0, 2))
 
@@ -205,7 +206,7 @@
     return cell, line, square, cross
 
 
-def step_kernel(first, last, *refs):
+def step_kernel(first, last, total_planes, *refs):
     refs = list(refs)
 
     def take(count):
@@ -222,21 +223,51 @@
     if not last:
         newstate_ref, sendup_ref, senddown_ref = take(3)
     if first:
-        (order_ref,) = take(1)
+        order_ref, places_ref = take(2)
     (
         old, new, velocity, force, boxes, sampled,
         shifts, stills, ring, middle, state,
-        in_sem, out_sem,
+        in_sem, out_sem, slot_sem, slots_smem,
     ) = refs
 
     for z in range(PLANES):
         pltpu.make_async_copy(moments_hbm.at[:, z], old.at[:, z + 1], in_sem.at[z]).start()
 
     if first:
+        home_ref, slots_ref = slots_ref, slots_smem
+        row = lax.broadcasted_iota(jnp.int32, (GROUP, 128), 0)
+        lane = lax.broadcasted_iota(jnp.int32, (GROUP, 128), 1)
+        last_part = tail_rows(0, 2, 1)[0]
+        values = (
+            below_ref[:, 256:LANES], up_ref[last_part], own_ref[:, 256:LANES],
+            down_ref[last_part], above_ref[:, 256:LANES],
+        )
+        edge = ANCHOR_LANE - 256
+        spots = jnp.zeros((GROUP, 128), F32)
+        for owner, value in enumerate(values):
+            column = jnp.broadcast_to(value[:, edge : edge + 1], (GROUP, 128))
+            spots = jnp.where(lane == row + owner * GROUP, column, spots)
+        spots = jnp.sum(spots, axis=0, keepdims=True).astype(jnp.int32)
+        lane = lane[0:1]
+        along = functools.reduce(
+            jnp.logical_or,
+            [
+                jnp.logical_and(lane >= owner * GROUP, lane < owner * GROUP + OWNED)
+                for owner in range(BLOCKS)
+            ],
+        )
+        half = total_planes // 2
+        local = ((spots - home_ref[0] + half) & (total_planes - 1)) - half
+        places_ref[...] = jnp.where(along, local, spots)
+        copy = pltpu.make_async_copy(places_ref, slots_smem, slot_sem.at[0])
+        copy.start()
+        copy.wait()
+
+    if first:
 
         def scan(slot, carry):
             count, spare = carry
-            above = slots_ref[slot_row(slot)]
+            above = slots_ref[0, slot_row(slot)]
             near = jnp.logical_and(above >= -BZ, above <= PLANES)
 
             @pl.when(near)
@@ -298,11 +329,11 @@
 
     def box_parts(slot):
         base = slot_row(slot)
-        above = slots_ref[base]
+        above = slots_ref[0, base]
         near = jnp.logical_and(above >= -BZ, above <= PLANES)
         above = jnp.where(near, above, PLANES + 1)
-        row = slots_ref[base + OWNED]
-        column = slots_ref[base + 2 * OWNED]
+        row = slots_ref[0, base + OWNED]
+        column = slots_ref[0, base + 2 * OWNED]
         lane = lax.broadcasted_iota(jnp.int32, (BXY, SIDE), 1)
         inside = lax.broadcasted_iota(jnp.int32, (BXY, SIDE), 0)
         hit = (((lane - column) & (SIDE - 1)) == inside).astype(F32).astype(BF16)
@@ -356,8 +387,7 @@
             pltpu.make_async_copy(moments_hbm.at[:, 0], old.at[:, z], in_sem.at[z - 1]).wait()
 
 
-        def collide_chunk(step, carry):
-            y = pl.multiple_of(step * WIDE, WIDE)
+        def collide_chunk(y):
             rows = pl.ds(y, WIDE)
             m = [old[f, z, rows] for f in range(FIELDS)]
             cell, line, square, cross = collide_rows(
@@ -380,9 +410,13 @@
                 shifts[12 + k, moved] = twice[k]
                 stills[k, rows] = 4.0 * even[0][k]
                 stills[3 + k, rows] = 4.0 * odd[0][k]
+
+        def collide_some(step, carry):
+            for n in range(UNROLL):
+                collide_chunk(pl.multiple_of(step * (WIDE * UNROLL), WIDE * UNROLL) + n * WIDE)
             return carry
 
-        lax.fori_loop(0, SIDE // WIDE, collide_chunk, 0)
+        lax.fori_loop(0, SIDE // (WIDE * UNROLL), collide_some, 0)
         for field in range(15):
             shifts[field, 7:8] = shifts[field, SIDE + 7 : SIDE + 8]
             shifts[field, SIDE + 8 : SIDE + 9] = shifts[field, 8:9]
@@ -490,7 +524,7 @@
         pltpu.make_async_copy(new.at[:, z + 2], out_hbm.at[:, z], out_sem.at[z]).wait()
 
 
-def advance(first, last, slots, high, low, moments, up, down, *rest):
+def advance(first, last, total_planes, slots, high, low, moments, up, down, *rest):
     square = (SIDE, SIDE)
     out_shape = [
         jax.ShapeDtypeStruct((FIELDS, PLANES) + square, F32),
@@ -507,6 +541,8 @@
     if first:
         out_shape.append(jax.ShapeDtypeStruct((ORDER,), jnp.int32))
         out_specs.append(SMEM)
+        out_shape.append(jax.ShapeDtypeStruct((1, 128), jnp.int32))
+        out_specs.append(VMEM)
     scratch = [
         pltpu.VMEM((FIELDS, PLANES + 2) + square, F32),
         pltpu.VMEM((FIELDS, PLANES + 2) + square, F32),
@@ -521,9 +557,11 @@
         pltpu.VMEM((ROWS, LANES), F32),
         pltpu.SemaphoreType.DMA((PLANES,)),
         pltpu.SemaphoreType.DMA((PLANES,)),
+        pltpu.SemaphoreType.DMA((1,)),
+        pltpu.SMEM((1, 128), jnp.int32),
     ]
     return pl.pallas_call(
-        functools.partial(step_kernel, first, last),
+        functools.partial(step_kernel, first, last, total_planes),
         out_shape=out_shape,
         in_specs=[SMEM, VMEM, VMEM, HBM, VMEM, VMEM] + [VMEM] * 2 + [VMEM if first else SMEM],
         out_specs=out_specs,
@@ -547,29 +585,17 @@
     above2 = shifted(small, -2)
     high, low = couple(jnp.pad(synthesis, ((0, 0), (0, LANES - COEFS))), spreading)
 
-    rows, edge = tail_rows(0, 2, 1)[0], ANCHOR_LANE - 256
-    places = jnp.concatenate(
-        [
-            below2[:, ANCHOR_LANE],
-            up[rows, edge],
-            small[:, ANCHOR_LANE],
-            down[rows, edge],
-            above2[:, ANCHOR_LANE],
-        ]
-    ).astype(jnp.int32)
-    half = total_planes // 2
-    local = (places - PLANES * lax.axis_index("gz") + half) % total_planes - half
-    slots = jnp.where(jnp.arange(ROWS, dtype=jnp.int32) % GROUP < OWNED, local, places)
+    slots = jnp.full((1,), PLANES * lax.axis_index("gz"), jnp.int32)
 
     rest = (small, below2, above2)
     for step in range(STEPS):
         last = step == STEPS - 1
-        results = advance(step == 0, last, slots, high, low, moments, up, down, *rest)
+        results = advance(step == 0, last, total_planes, slots, high, low, moments, up, down, *rest)
         moments, sums = results[:2]
         if not last:
             state, send_up, send_down = results[2:5]
             if step == 0:
-                order = results[5]
+                order, slots = results[5:]
             up, down = shifted(send_up, 1), shifted(send_down, -1)
             rest = (state, sums, order)
 

time: 120 us -> 109 us (0.908)
  starting transfers between devices: 42.5 us -> 37.4 us
  Pallas kernels: 47.3 us -> 44.7 us
  local copies, waits for them, and re-layouts: 4.92 us -> 2.52 us
    ppermute x11, starting transfers between devices: 42.5 us -> 37.4 us  [shifted(): lax.ppermute(block, 'gz', [((i - distance) % devices, i) for i in range(d...]
    pallas_call x3, Pallas kernels: 41.9 us -> 39.3 us  [advance(): pl.pallas_call(functools.partial(step_kernel, first, last, total_planes),...]
    slice x5 -> x0, local copies, waits for them, and re-layouts: 2.31 us -> none  [the longest x1 0.89 us: per_device(): up[rows, edge]]
  transfers between devices with their start and end apart: 11 -> 11, of which waited for: 6 -> 6; matrix products, arithmetic and copies ran while one was open for 1% -> 0% of each run, Pallas kernels for 2% -> 2%
where the time goes in v3:
time: 109 us
  Pallas kernels  44.7 us (41%)
  starting transfers between devices  37.4 us (34%)
  waiting for transfers between devices  23.2 us (21%)
  local copies, waits for them, and re-layouts  2.52 us (2%)
    pallas_call x3, Pallas kernels, advance(): pl.pallas_call(functools.partial(step_kernel, first, last, total_planes),...  39.3 us
    ppermute x11, starting transfers between devices, shifted(): lax.ppermute(block, 'gz', [((i - distance) % devices, i) for i in range(d...  37.4 us
    ppermute x11, waiting for transfers between devices, shifted(): lax.ppermute(block, 'gz', [((i - distance) % devices, i) for i in range(d...  23.2 us
    pallas_call x1, Pallas kernels, pack(): pl.pallas_call(pack_kernel, out_shape=(jax.ShapeDtypeStruct((GROUP, LANES...  3.21 us
    unnamed x9, local copies, waits for them, and re-layouts  2.46 us
    pallas_call x1, Pallas kernels, couple(): pl.pallas_call(couple_kernel, out_shape=(shape, shape), in_specs=[VMEM, V...  2.19 us
  transfers between devices with their start and end apart: 11, of which 6 were waited for; matrix products, arithmetic and copies ran while one was open for 0% of the time, Pallas kernels for 2%

profile of v3, /device:TPU:1, one launch (start us, length us, event | category | flops | bytes accessed | tf_op | source)
XLA Modules:
  0.0 109.2 jit_solution(17092531945366279304)
XLA Ops:
  0.6 3.2 %pack.1 = (f32[24,384]{1,0:T(8,128)}, f32[1224,128]{1,0:T(8,128)}, f32[1224,128]{1,0:T(8,128)}) custom-call(s32[3,8]{1,0:T(4,128)} %bitcast.10, f32[10,8,128,128]{3,2,1,0:T(8,128)} %refs_3_.1, f32[3,8,289]{2,1,0:T(8,128)} %bitcast.9), custom_call_target="tpu_custom_call" | custom-call | tf_op jit(solution)/shard_map/pack/pallas_call | solution.py:170
  3.9 3.1 %collective-permute-start = (f32[1224,128]{1,0:T(8,128)}, f32[1224,128]{1,0:T(8,128)}, u32[]{:S(2)}, u32[]{:S(2)}) collective-permute-start(f32[1224,128]{1,0:T(8,128)} %get-tuple-element.23), channel_id=1, source_target_pairs={{127,0},{0,1},{1,2},{2,3},{3,4},{4,5},{5,6},{6,7},{7,8},{8,9},{9,1... | collective-permute-start | bytes 1880072 | tf_op jit(solution)/shard_map/ppermute | solution.py:55
  6.9 0.0 collective-permute-start.1
  6.9 7.0 %collective-permute-start.3 = (f32[24,384]{1,0:T(8,128)}, f32[24,384]{1,0:T(8,128)S(1)}, u32[]{:S(2)}, u32[]{:S(2)}) collective-permute-start(f32[24,384]{1,0:T(8,128)} %get-tuple-element.25.refs_6_), channel_id=1, source_target_pairs={{2,0},{3,1},{4,2},{5,3},{6,4},{7,5},{8,6},{9,7},{10,8},{11,9},{12,... | collective-permute-start | bytes 110600 | tf_op jit(solution)/shard_map/ppermute | solution.py:55
  13.9 0.0 collective-permute-start.2
  13.9 0.3 copy.9
  14.2 0.0 copy-start
  14.2 0.1 pad.4.synthesis_ref
  14.3 0.0 copy-start.1
  14.3 2.2 %copy-done.1 = f32[512,2048]{1,0:T(8,128)S(1)} copy-done((f32[512,2048]{1,0:T(8,128)S(1)}, f32[512,2048]{1,0:T(8,128)}, u32[]{:S(2)}) %copy-start.1) | copy-done | bytes 4194328
  16.4 2.2 %couple.1 = (bf16[384,2048]{1,0:T(8,128)(2,1)S(1)}, bf16[384,2048]{1,0:T(8,128)(2,1)S(1)}) custom-call(f32[512,384]{1,0:T(8,128)S(1)} %pad.4.synthesis_ref, f32[512,2048]{1,0:T(8,128)S(1)} %copy-done.1), custom_call_target="tpu_custom_call" | custom-call | flops 2415919104 | bytes 8388608 | tf_op jit(solution)/shard_map/couple/pallas_call | solution.py:130
  18.6 0.0 collective-permute-done.3.refs_8_
  18.7 3.7 %collective-permute-done.2.refs_7_ = f32[24,384]{1,0:T(8,128)S(1)} collective-permute-done((f32[24,384]{1,0:T(8,128)}, f32[24,384]{1,0:T(8,128)S(1)}, u32[]{:S(2)}, u32[]{:S(2)}) %collective-permute-start.2) | collective-permute-done | bytes 36896 | tf_op jit(solution)/shard_map/ppermute | solution.py:55
  22.4 0.0 collective-permute-done.refs_4_
  22.4 0.0 collective-permute-done.1.refs_5_
  22.4 15.0 %first_step.1 = (f32[10,8,128,128]{3,2,1,0:T(8,128)}, f32[120,384]{1,0:T(8,128)S(1)}, f32[120,384]{1,0:T(8,128)S(1)}, f32[1320,128]{1,0:T(8,128)S(1)}, f32[1392,...) custom-call(s32[1]{0:T(128)} %bitcast.refs_0_, bf16[384,2048]{1,0:T(8,128)(2,1)S(1)} %get-tuple-element.21.refs_1_, ...), custom_call_target="tpu_custom_call" | custom-call | flops 400000000 | bytes 16777216 | tf_op jit(solution)/shard_map/first_step/pallas_call | solution.py:563
  37.4 2.4 %collective-permute-start.5 = (f32[1392,128]{1,0:T(8,128)S(1)}, f32[1392,128]{1,0:T(8,128)S(1)}, u32[]{:S(2)}, u32[]{:S(2)}) collective-permute-start(f32[1392,128]{1,0:T(8,128)S(1)} %get-tuple-element.29), channel_id=1, source_target_pairs={{1,0},{2,1},{3,2},{4,3},{5,4},{6,5},{7,6},{8,7},{9,8},{10,9},{11,1... | collective-permute-start | bytes 2138120 | tf_op jit(solution)/shard_map/ppermute | solution.py:55
  39.8 0.0 collective-permute-start.4
  39.8 7.7 %collective-permute-done.4.refs_4_ = f32[1320,128]{1,0:T(8,128)S(1)} collective-permute-done((f32[1320,128]{1,0:T(8,128)S(1)}, f32[1320,128]{1,0:T(8,128)S(1)}, u32[]{:S(2)}, u32[]{:S(2)}) %collective-permute-start.4) | collective-permute-done | bytes 675872 | tf_op jit(solution)/shard_map/ppermute | solution.py:55
  47.5 0.6 collective-permute-done.5.refs_5_
  48.1 12.2 %step.1 = (f32[10,8,128,128]{3,2,1,0:T(8,128)}, f32[120,384]{1,0:T(8,128)S(1)}, f32[120,384]{1,0:T(8,128)S(1)}, f32[1320,128]{1,0:T(8,128)S(1)}, f32[1392,128]{1,0:T(8,128)S(1)}) custom-call(s32[1,128]{1,0:T(1,128)S(1)} %get-tuple-element.26.refs_0_, bf16[384,2048]{1,0:T(8,128)(2,1)S(1)} %get-tuple-element.21.refs_1_, ...), custom_call_target="tpu_custom_call", output_to_operand_aliasing={{0}: (3, {})} | custom-call | flops 400000000 | bytes 16777216 | tf_op jit(solution)/shard_map/step/pallas_call | solution.py:563
  60.3 10.6 %collective-permute-start.7 = (f32[1392,128]{1,0:T(8,128)S(1)}, f32[1392,128]{1,0:T(8,128)S(1)}, u32[]{:S(2)}, u32[]{:S(2)}) collective-permute-start(f32[1392,128]{1,0:T(8,128)S(1)} %get-tuple-element.35), channel_id=1, source_target_pairs={{1,0},{2,1},{3,2},{4,3},{5,4},{6,5},{7,6},{8,7},{9,8},{10,9},{11,1... | collective-permute-start | bytes 2138120 | tf_op jit(solution)/shard_map/ppermute | solution.py:55
  70.9 0.0 collective-permute-start.6
  70.9 7.7 %collective-permute-done.6.refs_4_ = f32[1320,128]{1,0:T(8,128)S(1)} collective-permute-done((f32[1320,128]{1,0:T(8,128)S(1)}, f32[1320,128]{1,0:T(8,128)S(1)}, u32[]{:S(2)}, u32[]{:S(2)}) %collective-permute-start.6) | collective-permute-done | bytes 675872 | tf_op jit(solution)/shard_map/ppermute | solution.py:55
  78.7 0.0 collective-permute-done.7.refs_5_
  78.7 12.1 %last_step.1 = (f32[10,8,128,128]{3,2,1,0:T(8,128)}, f32[120,384]{1,0:T(8,128)S(1)}) custom-call(s32[1,128]{1,0:T(1,128)S(1)} %get-tuple-element.26.refs_0_, bf16[384,2048]{1,0:T(8,128)(2,1)S(1)} %get-tuple-element.21.refs_1_, bf16[384,2048]{1,0:T(8,128)(2,1)S(1)} %get-tuple-element.22.refs_2_, ...), custom_call_target="tpu_custom_call", output_to_operand_aliasing={{0}: (3, {})} | custom-call | flops 400000000 | bytes 16777216 | tf_op jit(solution)/shard_map/last_step/pallas_call | solution.py:563
  90.8 2.5 %collective-permute-start.8 = (f32[24,384]{1,0:T(8,128)S(1)}, f32[24,384]{1,0:T(8,128)S(1)}, u32[]{:S(2)}, u32[]{:S(2)}) collective-permute-start(f32[24,384]{1,0:T(8,128)S(1)} %get-tuple-element.40), channel_id=1, source_target_pairs={{127,0},{0,1},{1,2},{2,3},{3,4},{4,5},{5,6},{6,7},{7,8},{8,9},{9,1... | collective-permute-start | bytes 110600 | tf_op jit(solution)/shard_map/ppermute | solution.py:55
  93.3 11.8 %collective-permute-start.10 = (f32[24,384]{1,0:T(8,128)S(1)}, f32[24,384]{1,0:T(8,128)S(1)}, u32[]{:S(2)}, u32[]{:S(2)}) collective-permute-start(f32[24,384]{1,0:T(8,128)S(1)} %get-tuple-element.41), channel_id=1, source_target_pairs={{2,0},{3,1},{4,2},{5,3},{6,4},{7,5},{8,6},{9,7},{10,8},{11,9},{12,... | collective-permute-start | bytes 110600 | tf_op jit(solution)/shard_map/ppermute | solution.py:55
  105.1 0.0 collective-permute-start.9
  105.1 1.1 collective-permute-done.10
  106.2 2.3 %collective-permute-done.9 = f32[24,384]{1,0:T(8,128)S(1)} collective-permute-done((f32[24,384]{1,0:T(8,128)S(1)}, f32[24,384]{1,0:T(8,128)S(1)}, u32[]{:S(2)}, u32[]{:S(2)}) %collective-permute-start.9) | collective-permute-done | bytes 36896 | tf_op jit(solution)/shard_map/ppermute | solution.py:55
  108.5 0.6 fusion.1
  (8 shorter events, 0.0 us)
Async XLA Ops:
  0.6 13.3 %copy-start.2 = (f32[512,289]{0,1:T(8,128)S(1)}, f32[512,289]{0,1:T(8,128)}, u32[]{:S(2)}) copy-start(f32[512,289]{0,1:T(8,128)} %param.8) | copy-start | bytes 1775620
  3.9 18.5 %collective-permute-start = (f32[1224,128]{1,0:T(8,128)}, f32[1224,128]{1,0:T(8,128)}, u32[]{:S(2)}, u32[]{:S(2)}) collective-permute-start(f32[1224,128]{1,0:T(8,128)} %get-tuple-element.23), channel_id=1, source_target_pairs={{127,0},{0,1},{1,2},{2,3},{3,4},{4,5},{5,6},{6,7},{7,8},{8,9},{9,1... | collective-permute-start | bytes 1880072 | tf_op jit(solution)/shard_map/ppermute | solution.py:55
  6.9 15.4 %collective-permute-start.1 = (f32[1224,128]{1,0:T(8,128)}, f32[1224,128]{1,0:T(8,128)}, u32[]{:S(2)}, u32[]{:S(2)}) collective-permute-start(f32[1224,128]{1,0:T(8,128)} %get-tuple-element.24), channel_id=1, source_target_pairs={{1,0},{2,1},{3,2},{4,3},{5,4},{6,5},{7,6},{8,7},{9,8},{10,9},{11,1... | collective-permute-start | bytes 1880072 | tf_op jit(solution)/shard_map/ppermute | solution.py:55
  6.9 11.7 %collective-permute-start.3 = (f32[24,384]{1,0:T(8,128)}, f32[24,384]{1,0:T(8,128)S(1)}, u32[]{:S(2)}, u32[]{:S(2)}) collective-permute-start(f32[24,384]{1,0:T(8,128)} %get-tuple-element.25.refs_6_), channel_id=1, source_target_pairs={{2,0},{3,1},{4,2},{5,3},{6,4},{7,5},{8,6},{9,7},{10,8},{11,9},{12,... | collective-permute-start | bytes 110600 | tf_op jit(solution)/shard_map/ppermute | solution.py:55
  13.9 8.4 %collective-permute-start.2 = (f32[24,384]{1,0:T(8,128)}, f32[24,384]{1,0:T(8,128)S(1)}, u32[]{:S(2)}, u32[]{:S(2)}) collective-permute-start(f32[24,384]{1,0:T(8,128)} %get-tuple-element.25.refs_6_), channel_id=1, source_target_pairs={{126,0},{127,1},{0,2},{1,3},{2,4},{3,5},{4,6},{5,7},{6,8},{7,9},{8... | collective-permute-start | bytes 110600 | tf_op jit(solution)/shard_map/ppermute | solution.py:55
  14.2 8.2 %copy-start = (f32[24,384]{1,0:T(8,128)S(1)}, f32[24,384]{1,0:T(8,128)}, u32[]{:S(2)}) copy-start(f32[24,384]{1,0:T(8,128)} %get-tuple-element.25.refs_6_) | copy-start | bytes 110596
  14.3 2.2 %copy-start.1 = (f32[512,2048]{1,0:T(8,128)S(1)}, f32[512,2048]{1,0:T(8,128)}, u32[]{:S(2)}) copy-start(f32[512,2048]{1,0:T(8,128)} %spreading_ref.1) | copy-start | bytes 12582916
  37.4 10.7 %collective-permute-start.5 = (f32[1392,128]{1,0:T(8,128)S(1)}, f32[1392,128]{1,0:T(8,128)S(1)}, u32[]{:S(2)}, u32[]{:S(2)}) collective-permute-start(f32[1392,128]{1,0:T(8,128)S(1)} %get-tuple-element.29), channel_id=1, source_target_pairs={{1,0},{2,1},{3,2},{4,3},{5,4},{6,5},{7,6},{8,7},{9,8},{10,9},{11,1... | collective-permute-start | bytes 2138120 | tf_op jit(solution)/shard_map/ppermute | solution.py:55
  39.8 7.8 %collective-permute-start.4 = (f32[1320,128]{1,0:T(8,128)S(1)}, f32[1320,128]{1,0:T(8,128)S(1)}, u32[]{:S(2)}, u32[]{:S(2)}) collective-permute-start(f32[1320,128]{1,0:T(8,128)S(1)} %get-tuple-element.28), channel_id=1, source_target_pairs={{127,0},{0,1},{1,2},{2,3},{3,4},{4,5},{5,6},{6,7},{7,8},{8,9},{9,1... | collective-permute-start | bytes 2027528 | tf_op jit(solution)/shard_map/ppermute | solution.py:55
  60.3 18.4 %collective-permute-start.7 = (f32[1392,128]{1,0:T(8,128)S(1)}, f32[1392,128]{1,0:T(8,128)S(1)}, u32[]{:S(2)}, u32[]{:S(2)}) collective-permute-start(f32[1392,128]{1,0:T(8,128)S(1)} %get-tuple-element.35), channel_id=1, source_target_pairs={{1,0},{2,1},{3,2},{4,3},{5,4},{6,5},{7,6},{8,7},{9,8},{10,9},{11,1... | collective-permute-start | bytes 2138120 | tf_op jit(solution)/shard_map/ppermute | solution.py:55
  70.9 7.8 %collective-permute-start.6 = (f32[1320,128]{1,0:T(8,128)S(1)}, f32[1320,128]{1,0:T(8,128)S(1)}, u32[]{:S(2)}, u32[]{:S(2)}) collective-permute-start(f32[1320,128]{1,0:T(8,128)S(1)} %get-tuple-element.34), channel_id=1, source_target_pairs={{127,0},{0,1},{1,2},{2,3},{3,4},{4,5},{5,6},{6,7},{7,8},{8,9},{9,1... | collective-permute-start | bytes 2027528 | tf_op jit(solution)/shard_map/ppermute | solution.py:55
  78.7 29.9 %copy-start.3 = (f32[8,3,289]{2,0,1:T(8,128)S(1)}, f32[8,3,289]{2,0,1:T(8,128)}, u32[]{:S(2)}) copy-start(f32[8,3,289]{2,0,1:T(8,128)} %param.6) | copy-start | bytes 83236
  90.8 14.3 %collective-permute-start.8 = (f32[24,384]{1,0:T(8,128)S(1)}, f32[24,384]{1,0:T(8,128)S(1)}, u32[]{:S(2)}, u32[]{:S(2)}) collective-permute-start(f32[24,384]{1,0:T(8,128)S(1)} %get-tuple-element.40), channel_id=1, source_target_pairs={{127,0},{0,1},{1,2},{2,3},{3,4},{4,5},{5,6},{6,7},{7,8},{8,9},{9,1... | collective-permute-start | bytes 110600 | tf_op jit(solution)/shard_map/ppermute | solution.py:55
  93.3 12.9 %collective-permute-start.10 = (f32[24,384]{1,0:T(8,128)S(1)}, f32[24,384]{1,0:T(8,128)S(1)}, u32[]{:S(2)}, u32[]{:S(2)}) collective-permute-start(f32[24,384]{1,0:T(8,128)S(1)} %get-tuple-element.41), channel_id=1, source_target_pairs={{2,0},{3,1},{4,2},{5,3},{6,4},{7,5},{8,6},{9,7},{10,8},{11,9},{12,... | collective-permute-start | bytes 110600 | tf_op jit(solution)/shard_map/ppermute | solution.py:55
  105.1 3.4 %collective-permute-start.9 = (f32[24,384]{1,0:T(8,128)S(1)}, f32[24,384]{1,0:T(8,128)S(1)}, u32[]{:S(2)}, u32[]{:S(2)}) collective-permute-start(f32[24,384]{1,0:T(8,128)S(1)} %get-tuple-element.42), channel_id=1, source_target_pairs={{1,0},{2,1},{3,2},{4,3},{5,4},{6,5},{7,6},{8,7},{9,8},{10,9},{11,1... | collective-permute-start | bytes 110600 | tf_op jit(solution)/shard_map/ppermute | solution.py:55

commit v4 on v3

--- a/solution.py
+++ b/solution.py
@@ -270,13 +270,10 @@
             above = slots_ref[0, slot_row(slot)]
             near = jnp.logical_and(above >= -BZ, above <= PLANES)
 
-            @pl.when(near)
-            def _():
-                order_ref[count] = slot
-
+            order_ref[count] = slot
             return count + near.astype(jnp.int32), jnp.where(near, spare, slot)
 
-        count, spare = lax.fori_loop(0, SLOTS, scan, (jnp.int32(0), jnp.int32(0)))
+        count, spare = lax.fori_loop(0, SLOTS, scan, (jnp.int32(0), jnp.int32(0)), unroll=8)
         for n in range(BATCH - 1):
             order_ref[count + n] = spare
         order_ref[ORDER - 1] = (count + BATCH - 1) // BATCH
@@ -381,10 +378,67 @@
 
     lax.fori_loop(0, PLANES + 2, fold, 0)
 
+    def stream_edge(z, sign):
+        add = jnp.add if sign > 0 else jnp.subtract
+        for step in range(SIDE // WIDE):
+            y = step * WIDE
+            rows = slice(y, y + WIDE)
+            m = [old[f, z, rows] for f in range(FIELDS)]
+            starts = [(c * DEPTH + z + BZ - 1) * PITCH + y for c in range(3)]
+            cell, line, square, cross = collide_rows(m, [force[n : n + WIDE] for n in starts])
+            even = [
+                spread_x(add(cell + square[0], line[0]), add(line[2], cross[1]), square[2]),
+                spread_x(add(line[1], cross[0]), cross[2], None),
+                spread_x(square[1], None, None),
+            ]
+            moved = slice(y + 8, y + 8 + WIDE)
+            for k in range(3):
+                ends = even[0][k] + even[2][k]
+                shifts[k, moved] = ends + even[1][k]
+                shifts[3 + k, moved] = ends - even[1][k]
+                stills[k, rows] = 4.0 * even[0][k]
+        for field in range(6):
+            shifts[field, 7:8] = shifts[field, SIDE + 7 : SIDE + 8]
+            shifts[field, SIDE + 8 : SIDE + 9] = shifts[field, 8:9]
+        for step in range(SIDE // CHUNK):
+            y = step * CHUNK
+            rows = slice(y, y + CHUNK)
+            even = {}
+            for k in range(3):
+                up, down = shifts[k, y + 7 : y + 7 + CHUNK], shifts[3 + k, y + 9 : y + 9 + CHUNK]
+                both = up + down
+                even[0, k] = stills[k, rows] + both
+                even[1, k] = up - down
+                even[2, k] = both
+            if sign > 0:
+                for n, key in enumerate(JK):
+                    ring[z % 2, n, rows] = even[key]
+            else:
+                finish(z, z % 2, PLANES - 1, y, {key: even[key] for key in JK})
+
+    def finish(z, parity, inner, y, over):
+        rows = slice(y, y + CHUNK)
+        total, difference, centre = {}, {}, {}
+        for n, key in enumerate(JK):
+            under = ring[parity, n, rows]
+            total[key] = under + over[key]
+            difference[key] = under - over[key]
+            centre[key] = middle[n, rows] + total[key]
+        flow = (difference[0, 0], centre[1, 0], centre[0, 1])
+        results = (
+            centre[0, 0], *flow, total[0, 0], centre[2, 0], centre[0, 2],
+            difference[1, 0], difference[0, 1], centre[1, 1],
+        )
+        for f, value in enumerate(results):
+            new[f, z, rows] = value
+        for c in range(3):
+            start = (c * DEPTH + inner + BZ) * PITCH
+            velocity[pl.ds(start + y, CHUNK)] = flow[c]
+            if y == 0:
+                velocity[pl.ds(start + SIDE, BXY)] = flow[c]
+
     def stream_plane(z, carry):
-        @pl.when(jnp.logical_and(z >= 1, z <= PLANES))
-        def _():
-            pltpu.make_async_copy(moments_hbm.at[:, 0], old.at[:, z], in_sem.at[z - 1]).wait()
+        pltpu.make_async_copy(moments_hbm.at[:, 0], old.at[:, z], in_sem.at[z - 1]).wait()
 
 
         def collide_chunk(y):
@@ -442,28 +496,11 @@
                         target[1, k] = up - down
                     if k < 1:
                         target[2, k] = both
-            total, difference, centre = {}, {}, {}
+            ends = {key: even[key] + twice[key] for key in JK}
+            finish(z, parity, inner, y, {key: ends[key] - odd[key] for key in JK})
             for n, key in enumerate(JK):
-                ends = even[key] + twice[key]
-                under = ring[parity, n, rows]
-                over = ends - odd[key]
-                total[key] = under + over
-                difference[key] = under - over
-                centre[key] = middle[n, rows] + total[key]
-                ring[parity, n, rows] = ends + odd[key]
+                ring[parity, n, rows] = ends[key] + odd[key]
                 middle[n, rows] = 4.0 * even[key]
-            flow = (difference[0, 0], centre[1, 0], centre[0, 1])
-            results = (
-                centre[0, 0], *flow, total[0, 0], centre[2, 0], centre[0, 2],
-                difference[1, 0], difference[0, 1], centre[1, 1],
-            )
-            for f, value in enumerate(results):
-                new[f, z, rows] = value
-            for c in range(3):
-                start = (c * DEPTH + inner + BZ) * PITCH
-                velocity[pl.ds(start + y, CHUNK)] = flow[c]
-                if step == 0:
-                    velocity[pl.ds(start + SIDE, BXY)] = flow[c]
 
         @pl.when(z >= 2)
         def _():
@@ -471,7 +508,10 @@
 
         return carry
 
-    lax.fori_loop(0, PLANES + 2, stream_plane, 0)
+    stream_edge(0, 1)
+    lax.fori_loop(1, PLANES + 1, stream_plane, 0)
+    stream_edge(PLANES + 1, -1)
+    pltpu.make_async_copy(new.at[:, PLANES + 1], out_hbm.at[:, PLANES - 1], out_sem.at[PLANES - 1]).start()
 
     if not last:
         write_plane(sendup_ref, lambda f: new[f, PLANES + 1])

time: 109 us -> 108 us (level)
  Pallas kernels: 44.7 us -> 43.1 us
    pallas_call x3, Pallas kernels: 39.3 us -> 37.7 us  [advance(): pl.pallas_call(functools.partial(step_kernel, first, last, total_planes),...]
where the time goes in v4:
time: 108 us
  Pallas kernels  43.1 us (40%)
  starting transfers between devices  37.6 us (35%)
  waiting for transfers between devices  23.2 us (21%)
  local copies, waits for them, and re-layouts  2.52 us (2%)
    pallas_call x3, Pallas kernels, advance(): pl.pallas_call(functools.partial(step_kernel, first, last, total_planes),...  37.7 us
    ppermute x11, starting transfers between devices, shifted(): lax.ppermute(block, 'gz', [((i - distance) % devices, i) for i in range(d...  37.6 us
    ppermute x11, waiting for transfers between devices, shifted(): lax.ppermute(block, 'gz', [((i - distance) % devices, i) for i in range(d...  23.2 us
    pallas_call x1, Pallas kernels, pack(): pl.pallas_call(pack_kernel, out_shape=(jax.ShapeDtypeStruct((GROUP, LANES...  3.21 us
    unnamed x9, local copies, waits for them, and re-layouts  2.46 us
    pallas_call x1, Pallas kernels, couple(): pl.pallas_call(couple_kernel, out_shape=(shape, shape), in_specs=[VMEM, V...  2.19 us
  transfers between devices with their start and end apart: 11, of which 6 were waited for; matrix products, arithmetic and copies ran while one was open for 0% of the time, Pallas kernels for 2%

profile of v4, /device:TPU:1, one launch (start us, length us, event | category | flops | bytes accessed | tf_op | source)
XLA Modules:
  0.0 107.8 jit_solution(5688519748585538510)
XLA Ops:
  0.6 3.2 %pack.1 = (f32[24,384]{1,0:T(8,128)}, f32[1224,128]{1,0:T(8,128)}, f32[1224,128]{1,0:T(8,128)}) custom-call(s32[3,8]{1,0:T(4,128)} %bitcast.10, f32[10,8,128,128]{3,2,1,0:T(8,128)} %refs_3_.1, f32[3,8,289]{2,1,0:T(8,128)} %bitcast.9), custom_call_target="tpu_custom_call" | custom-call | tf_op jit(solution)/shard_map/pack/pallas_call | solution.py:170
  3.9 3.1 %collective-permute-start = (f32[1224,128]{1,0:T(8,128)}, f32[1224,128]{1,0:T(8,128)}, u32[]{:S(2)}, u32[]{:S(2)}) collective-permute-start(f32[1224,128]{1,0:T(8,128)} %get-tuple-element.23), channel_id=1, source_target_pairs={{127,0},{0,1},{1,2},{2,3},{3,4},{4,5},{5,6},{6,7},{7,8},{8,9},{9,1... | collective-permute-start | bytes 1880072 | tf_op jit(solution)/shard_map/ppermute | solution.py:55
  6.9 0.0 collective-permute-start.1
  6.9 7.0 %collective-permute-start.3 = (f32[24,384]{1,0:T(8,128)}, f32[24,384]{1,0:T(8,128)S(1)}, u32[]{:S(2)}, u32[]{:S(2)}) collective-permute-start(f32[24,384]{1,0:T(8,128)} %get-tuple-element.25.refs_6_), channel_id=1, source_target_pairs={{2,0},{3,1},{4,2},{5,3},{6,4},{7,5},{8,6},{9,7},{10,8},{11,9},{12,... | collective-permute-start | bytes 110600 | tf_op jit(solution)/shard_map/ppermute | solution.py:55
  13.9 0.0 collective-permute-start.2
  13.9 0.3 copy.9
  14.2 0.0 copy-start
  14.2 0.1 pad.4.synthesis_ref
  14.3 0.0 copy-start.1
  14.3 2.2 %copy-done.1 = f32[512,2048]{1,0:T(8,128)S(1)} copy-done((f32[512,2048]{1,0:T(8,128)S(1)}, f32[512,2048]{1,0:T(8,128)}, u32[]{:S(2)}) %copy-start.1) | copy-done | bytes 4194328
  16.4 2.2 %couple.1 = (bf16[384,2048]{1,0:T(8,128)(2,1)S(1)}, bf16[384,2048]{1,0:T(8,128)(2,1)S(1)}) custom-call(f32[512,384]{1,0:T(8,128)S(1)} %pad.4.synthesis_ref, f32[512,2048]{1,0:T(8,128)S(1)} %copy-done.1), custom_call_target="tpu_custom_call" | custom-call | flops 2415919104 | bytes 8388608 | tf_op jit(solution)/shard_map/couple/pallas_call | solution.py:130
  18.6 0.0 collective-permute-done.3.refs_8_
  18.7 3.7 %collective-permute-done.2.refs_7_ = f32[24,384]{1,0:T(8,128)S(1)} collective-permute-done((f32[24,384]{1,0:T(8,128)}, f32[24,384]{1,0:T(8,128)S(1)}, u32[]{:S(2)}, u32[]{:S(2)}) %collective-permute-start.2) | collective-permute-done | bytes 36896 | tf_op jit(solution)/shard_map/ppermute | solution.py:55
  22.4 0.0 collective-permute-done.refs_4_
  22.4 0.0 collective-permute-done.1.refs_5_
  22.4 14.2 %first_step.1 = (f32[10,8,128,128]{3,2,1,0:T(8,128)}, f32[120,384]{1,0:T(8,128)S(1)}, f32[120,384]{1,0:T(8,128)S(1)}, f32[1320,128]{1,0:T(8,128)S(1)}, f32[1392,...) custom-call(s32[1]{0:T(128)} %bitcast.refs_0_, bf16[384,2048]{1,0:T(8,128)(2,1)S(1)} %get-tuple-element.21.refs_1_, ...), custom_call_target="tpu_custom_call" | custom-call | flops 400000000 | bytes 16777216 | tf_op jit(solution)/shard_map/first_step/pallas_call | solution.py:603
  36.6 2.4 %collective-permute-start.5 = (f32[1392,128]{1,0:T(8,128)S(1)}, f32[1392,128]{1,0:T(8,128)S(1)}, u32[]{:S(2)}, u32[]{:S(2)}) collective-permute-start(f32[1392,128]{1,0:T(8,128)S(1)} %get-tuple-element.29), channel_id=1, source_target_pairs={{1,0},{2,1},{3,2},{4,3},{5,4},{6,5},{7,6},{8,7},{9,8},{10,9},{11,1... | collective-permute-start | bytes 2138120 | tf_op jit(solution)/shard_map/ppermute | solution.py:55
  39.0 0.0 collective-permute-start.4
  39.0 7.7 %collective-permute-done.4.refs_4_ = f32[1320,128]{1,0:T(8,128)S(1)} collective-permute-done((f32[1320,128]{1,0:T(8,128)S(1)}, f32[1320,128]{1,0:T(8,128)S(1)}, u32[]{:S(2)}, u32[]{:S(2)}) %collective-permute-start.4) | collective-permute-done | bytes 675872 | tf_op jit(solution)/shard_map/ppermute | solution.py:55
  46.7 0.6 collective-permute-done.5.refs_5_
  47.3 11.8 %step.1 = (f32[10,8,128,128]{3,2,1,0:T(8,128)}, f32[120,384]{1,0:T(8,128)S(1)}, f32[120,384]{1,0:T(8,128)S(1)}, f32[1320,128]{1,0:T(8,128)S(1)}, f32[1392,128]{1,0:T(8,128)S(1)}) custom-call(s32[1,128]{1,0:T(1,128)S(1)} %get-tuple-element.26.refs_0_, bf16[384,2048]{1,0:T(8,128)(2,1)S(1)} %get-tuple-element.21.refs_1_, ...), custom_call_target="tpu_custom_call", output_to_operand_aliasing={{0}: (3, {})} | custom-call | flops 400000000 | bytes 16777216 | tf_op jit(solution)/shard_map/step/pallas_call | solution.py:603
  59.1 10.8 %collective-permute-start.7 = (f32[1392,128]{1,0:T(8,128)S(1)}, f32[1392,128]{1,0:T(8,128)S(1)}, u32[]{:S(2)}, u32[]{:S(2)}) collective-permute-start(f32[1392,128]{1,0:T(8,128)S(1)} %get-tuple-element.35), channel_id=1, source_target_pairs={{1,0},{2,1},{3,2},{4,3},{5,4},{6,5},{7,6},{8,7},{9,8},{10,9},{11,1... | collective-permute-start | bytes 2138120 | tf_op jit(solution)/shard_map/ppermute | solution.py:55
  69.9 0.0 collective-permute-start.6
  69.9 7.7 %collective-permute-done.6.refs_4_ = f32[1320,128]{1,0:T(8,128)S(1)} collective-permute-done((f32[1320,128]{1,0:T(8,128)S(1)}, f32[1320,128]{1,0:T(8,128)S(1)}, u32[]{:S(2)}, u32[]{:S(2)}) %collective-permute-start.6) | collective-permute-done | bytes 675872 | tf_op jit(solution)/shard_map/ppermute | solution.py:55
  77.7 11.7 %last_step.1 = (f32[10,8,128,128]{3,2,1,0:T(8,128)}, f32[120,384]{1,0:T(8,128)S(1)}) custom-call(s32[1,128]{1,0:T(1,128)S(1)} %get-tuple-element.26.refs_0_, bf16[384,2048]{1,0:T(8,128)(2,1)S(1)} %get-tuple-element.21.refs_1_, bf16[384,2048]{1,0:T(8,128)(2,1)S(1)} %get-tuple-element.22.refs_2_, ...), custom_call_target="tpu_custom_call", output_to_operand_aliasing={{0}: (3, {})} | custom-call | flops 400000000 | bytes 16777216 | tf_op jit(solution)/shard_map/last_step/pallas_call | solution.py:603
  89.4 2.5 %collective-permute-start.8 = (f32[24,384]{1,0:T(8,128)S(1)}, f32[24,384]{1,0:T(8,128)S(1)}, u32[]{:S(2)}, u32[]{:S(2)}) collective-permute-start(f32[24,384]{1,0:T(8,128)S(1)} %get-tuple-element.40), channel_id=1, source_target_pairs={{127,0},{0,1},{1,2},{2,3},{3,4},{4,5},{5,6},{6,7},{7,8},{8,9},{9,1... | collective-permute-start | bytes 110600 | tf_op jit(solution)/shard_map/ppermute | solution.py:55
  91.9 11.8 %collective-permute-start.10 = (f32[24,384]{1,0:T(8,128)S(1)}, f32[24,384]{1,0:T(8,128)S(1)}, u32[]{:S(2)}, u32[]{:S(2)}) collective-permute-start(f32[24,384]{1,0:T(8,128)S(1)} %get-tuple-element.41), channel_id=1, source_target_pairs={{2,0},{3,1},{4,2},{5,3},{6,4},{7,5},{8,6},{9,7},{10,8},{11,9},{12,... | collective-permute-start | bytes 110600 | tf_op jit(solution)/shard_map/ppermute | solution.py:55
  103.7 0.0 collective-permute-start.9
  103.7 0.0 collective-permute-done.8
  103.7 1.1 collective-permute-done.10
  104.8 2.3 %collective-permute-done.9 = f32[24,384]{1,0:T(8,128)S(1)} collective-permute-done((f32[24,384]{1,0:T(8,128)S(1)}, f32[24,384]{1,0:T(8,128)S(1)}, u32[]{:S(2)}, u32[]{:S(2)}) %collective-permute-start.9) | collective-permute-done | bytes 36896 | tf_op jit(solution)/shard_map/ppermute | solution.py:55
  107.1 0.6 fusion.1
  (8 shorter events, 0.0 us)
Async XLA Ops:
  0.6 13.3 %copy-start.2 = (f32[512,289]{0,1:T(8,128)S(1)}, f32[512,289]{0,1:T(8,128)}, u32[]{:S(2)}) copy-start(f32[512,289]{0,1:T(8,128)} %param.8) | copy-start | bytes 1775620
  3.9 18.5 %collective-permute-start = (f32[1224,128]{1,0:T(8,128)}, f32[1224,128]{1,0:T(8,128)}, u32[]{:S(2)}, u32[]{:S(2)}) collective-permute-start(f32[1224,128]{1,0:T(8,128)} %get-tuple-element.23), channel_id=1, source_target_pairs={{127,0},{0,1},{1,2},{2,3},{3,4},{4,5},{5,6},{6,7},{7,8},{8,9},{9,1... | collective-permute-start | bytes 1880072 | tf_op jit(solution)/shard_map/ppermute | solution.py:55
  6.9 15.4 %collective-permute-start.1 = (f32[1224,128]{1,0:T(8,128)}, f32[1224,128]{1,0:T(8,128)}, u32[]{:S(2)}, u32[]{:S(2)}) collective-permute-start(f32[1224,128]{1,0:T(8,128)} %get-tuple-element.24), channel_id=1, source_target_pairs={{1,0},{2,1},{3,2},{4,3},{5,4},{6,5},{7,6},{8,7},{9,8},{10,9},{11,1... | collective-permute-start | bytes 1880072 | tf_op jit(solution)/shard_map/ppermute | solution.py:55
  6.9 11.7 %collective-permute-start.3 = (f32[24,384]{1,0:T(8,128)}, f32[24,384]{1,0:T(8,128)S(1)}, u32[]{:S(2)}, u32[]{:S(2)}) collective-permute-start(f32[24,384]{1,0:T(8,128)} %get-tuple-element.25.refs_6_), channel_id=1, source_target_pairs={{2,0},{3,1},{4,2},{5,3},{6,4},{7,5},{8,6},{9,7},{10,8},{11,9},{12,... | collective-permute-start | bytes 110600 | tf_op jit(solution)/shard_map/ppermute | solution.py:55
  13.9 8.4 %collective-permute-start.2 = (f32[24,384]{1,0:T(8,128)}, f32[24,384]{1,0:T(8,128)S(1)}, u32[]{:S(2)}, u32[]{:S(2)}) collective-permute-start(f32[24,384]{1,0:T(8,128)} %get-tuple-element.25.refs_6_), channel_id=1, source_target_pairs={{126,0},{127,1},{0,2},{1,3},{2,4},{3,5},{4,6},{5,7},{6,8},{7,9},{8... | collective-permute-start | bytes 110600 | tf_op jit(solution)/shard_map/ppermute | solution.py:55
  14.2 8.2 %copy-start = (f32[24,384]{1,0:T(8,128)S(1)}, f32[24,384]{1,0:T(8,128)}, u32[]{:S(2)}) copy-start(f32[24,384]{1,0:T(8,128)} %get-tuple-element.25.refs_6_) | copy-start | bytes 110596
  14.3 2.2 %copy-start.1 = (f32[512,2048]{1,0:T(8,128)S(1)}, f32[512,2048]{1,0:T(8,128)}, u32[]{:S(2)}) copy-start(f32[512,2048]{1,0:T(8,128)} %spreading_ref.1) | copy-start | bytes 12582916
  36.6 10.7 %collective-permute-start.5 = (f32[1392,128]{1,0:T(8,128)S(1)}, f32[1392,128]{1,0:T(8,128)S(1)}, u32[]{:S(2)}, u32[]{:S(2)}) collective-permute-start(f32[1392,128]{1,0:T(8,128)S(1)} %get-tuple-element.29), channel_id=1, source_target_pairs={{1,0},{2,1},{3,2},{4,3},{5,4},{6,5},{7,6},{8,7},{9,8},{10,9},{11,1... | collective-permute-start | bytes 2138120 | tf_op jit(solution)/shard_map/ppermute | solution.py:55
  39.0 7.8 %collective-permute-start.4 = (f32[1320,128]{1,0:T(8,128)S(1)}, f32[1320,128]{1,0:T(8,128)S(1)}, u32[]{:S(2)}, u32[]{:S(2)}) collective-permute-start(f32[1320,128]{1,0:T(8,128)S(1)} %get-tuple-element.28), channel_id=1, source_target_pairs={{127,0},{0,1},{1,2},{2,3},{3,4},{4,5},{5,6},{6,7},{7,8},{8,9},{9,1... | collective-permute-start | bytes 2027528 | tf_op jit(solution)/shard_map/ppermute | solution.py:55
  59.1 18.5 %collective-permute-start.7 = (f32[1392,128]{1,0:T(8,128)S(1)}, f32[1392,128]{1,0:T(8,128)S(1)}, u32[]{:S(2)}, u32[]{:S(2)}) collective-permute-start(f32[1392,128]{1,0:T(8,128)S(1)} %get-tuple-element.35), channel_id=1, source_target_pairs={{1,0},{2,1},{3,2},{4,3},{5,4},{6,5},{7,6},{8,7},{9,8},{10,9},{11,1... | collective-permute-start | bytes 2138120 | tf_op jit(solution)/shard_map/ppermute | solution.py:55
  69.9 7.8 %collective-permute-start.6 = (f32[1320,128]{1,0:T(8,128)S(1)}, f32[1320,128]{1,0:T(8,128)S(1)}, u32[]{:S(2)}, u32[]{:S(2)}) collective-permute-start(f32[1320,128]{1,0:T(8,128)S(1)} %get-tuple-element.34), channel_id=1, source_target_pairs={{127,0},{0,1},{1,2},{2,3},{3,4},{4,5},{5,6},{6,7},{7,8},{8,9},{9,1... | collective-permute-start | bytes 2027528 | tf_op jit(solution)/shard_map/ppermute | solution.py:55
  77.7 29.5 %copy-start.3 = (f32[8,3,289]{2,0,1:T(8,128)S(1)}, f32[8,3,289]{2,0,1:T(8,128)}, u32[]{:S(2)}) copy-start(f32[8,3,289]{2,0,1:T(8,128)} %param.6) | copy-start | bytes 83236
  89.4 14.4 %collective-permute-start.8 = (f32[24,384]{1,0:T(8,128)S(1)}, f32[24,384]{1,0:T(8,128)S(1)}, u32[]{:S(2)}, u32[]{:S(2)}) collective-permute-start(f32[24,384]{1,0:T(8,128)S(1)} %get-tuple-element.40), channel_id=1, source_target_pairs={{127,0},{0,1},{1,2},{2,3},{3,4},{4,5},{5,6},{6,7},{7,8},{8,9},{9,1... | collective-permute-start | bytes 110600 | tf_op jit(solution)/shard_map/ppermute | solution.py:55
  91.9 12.9 %collective-permute-start.10 = (f32[24,384]{1,0:T(8,128)S(1)}, f32[24,384]{1,0:T(8,128)S(1)}, u32[]{:S(2)}, u32[]{:S(2)}) collective-permute-start(f32[24,384]{1,0:T(8,128)S(1)} %get-tuple-element.41), channel_id=1, source_target_pairs={{2,0},{3,1},{4,2},{5,3},{6,4},{7,5},{8,6},{9,7},{10,8},{11,9},{12,... | collective-permute-start | bytes 110600 | tf_op jit(solution)/shard_map/ppermute | solution.py:55
  103.7 3.4 %collective-permute-start.9 = (f32[24,384]{1,0:T(8,128)S(1)}, f32[24,384]{1,0:T(8,128)S(1)}, u32[]{:S(2)}, u32[]{:S(2)}) collective-permute-start(f32[24,384]{1,0:T(8,128)S(1)} %get-tuple-element.42), channel_id=1, source_target_pairs={{1,0},{2,1},{3,2},{4,3},{5,4},{6,5},{7,6},{8,7},{9,8},{10,9},{11,1... | collective-permute-start | bytes 110600 | tf_op jit(solution)/shard_map/ppermute | solution.py:55
